TPU v7x, 32 devices: a whole 2x2x4 slice. The times are simulated.
32 devices in a mesh: head: 4 (over y, x), blk: 8 (over z, core).
Axes of the slice: x: 2, y: 2, z: 4, core: 2. Of those that a mesh axis runs over, the one named last changes fastest.
Arguments:
- tokens: bfloat16 [4096, 2048], P(('head', 'blk')), may hold values from -6 to 6
- query_weight: bfloat16 [2048, 2048], P(('head', 'blk')), may hold values from -0.125 to 0.125
- key_weight: bfloat16 [2048, 2048], P(('head', 'blk')), may hold values from -0.125 to 0.125
- value_weight: bfloat16 [2048, 2048], P(('head', 'blk')), may hold values from -0.125 to 0.125
- output_weight: bfloat16 [2048, 2048], P(('head', 'blk')), may hold values from -4 to 4
- mixing_gain: bfloat16 [2048], P(('head', 'blk')), may hold values from 0.5 to 1.5
- query_gain: bfloat16 [2048], P(('head', 'blk')), may hold values from 0.5 to 1.5
- key_gain: bfloat16 [2048], P(('head', 'blk')), may hold values from 0.5 to 1.5
- routing_gain: bfloat16 [2048], P(('head', 'blk')), may hold values from 0.5 to 1.5
- router_weight: bfloat16 [2048, 16], P(('head', 'blk')), may hold values from -0.125 to 0.125
- gate_weight: bfloat16 [16, 2048, 1024], P('blk', 'head'), may hold values from -0.125 to 0.125
- up_weight: bfloat16 [16, 2048, 1024], P('blk', 'head'), may hold values from -0.125 to 0.125
- down_weight: bfloat16 [16, 1024, 2048], P('blk', 'head'), may hold values from -3 to 3
- seq_lengths: int32 [3], replicated, may hold values from 1024 to 2048, as said below
- dealt_order: int32 [4096], replicated, may hold values from 0 to 4095, as said below
- expert_routes: int32 [4096, 8], P(('head', 'blk')), may hold values from 0 to 15, all different within a row
- slot_order: int32 [4096, 8], P(('head', 'blk')), may hold values from 0 to 1023, as said below
- cotangent: bfloat16 [4096, 2048], P(('head', 'blk')), may hold values from -6 to 6
Outputs:
- block_output: bfloat16 [4096, 2048], P(('head', 'blk'))
- tokens_grad: float32 [4096, 2048], P(('head', 'blk'))
- query_grad: float32 [2048, 2048], P(('head', 'blk'))
- key_grad: float32 [2048, 2048], P(('head', 'blk'))
- value_grad: float32 [2048, 2048], P(('head', 'blk'))
- output_grad: float32 [2048, 2048], P(('head', 'blk'))
- mixing_grad: float32 [2048], P(('head', 'blk'))
- querynorm_grad: float32 [2048], P(('head', 'blk'))
- keynorm_grad: float32 [2048], P(('head', 'blk'))
- routing_grad: float32 [2048], P(('head', 'blk'))
- router_grad: float32 [2048, 16], P(('head', 'blk'))
- gate_grad: float32 [16, 2048, 1024], P('blk', 'head')
- up_grad: float32 [16, 2048, 1024], P('blk', 'head')
- down_grad: float32 [16, 1024, 2048], P('blk', 'head')
Inputs may be any that keep to these rules, and one draw needn't show every extreme that they name: `seq_lengths`: 3 lengths summing to 4096, the largest exactly 2048. `dealt_order`: a permutation of the stream; the rows of the devices of one index of blk, taken in head order, are two runs of 256 consecutive stream tokens, runs c and 15 - c. `expert_routes`: each row names 8 different experts. `slot_order`: within each aligned block of 128 rows the entries are 0 to 1023, each once.
All inputs are finite; a program needn't handle non-finite values.
Results may differ from a plain program's by a relative error of at most 0.022.
Values may be sent and summed in bfloat16 or wider, within the bound.
No kernel may reach another device: no remote copies, remote signals or barrier semaphores. Data moves between devices by JAX's collectives and lax.ppermute only.
A program may use at most 320 MiB of HBM per device.

v0:
```python
from functools import partial
import math

import jax
import jax.numpy as jnp
from jax import lax
from jax.sharding import PartitionSpec as P

HDIM = 128


norm_eps = 1e-05
rope_base = 10000.0


def as_sent(array):

    def short(part):
        return part.astype(jnp.bfloat16) if part.dtype == jnp.float32 else part

    return jax.tree.map(short, array)


def rmsnorm(value, gain):
    factor = lax.rsqrt(jnp.mean(value * value, axis=-1, keepdims=True) + norm_eps)
    return value * factor * gain


def rotate(value, position, head_size):
    half = head_size // 2
    heads = value.shape[1] // head_size
    freqs = rope_base ** (-(jnp.arange(half, dtype=jnp.float32) * 2.0) / head_size)
    angles = position.astype(jnp.float32)[:, None] * freqs[None, :]
    cosine = jnp.cos(angles)[:, None, :]
    sine_part = jnp.sin(angles)[:, None, :]
    shaped = value.reshape(value.shape[0], heads, head_size)
    former = shaped[:, :, :half]
    latter = shaped[:, :, half:]
    turned = jnp.concatenate(
        [former * cosine - latter * sine_part, latter * cosine + former * sine_part], axis=-1
    )
    return turned.reshape(value.shape)


def norm_rotate(raw, gain, position, head_size):
    return rotate(rmsnorm(raw, gain), position, head_size)


def stream_layout(seq_lengths, stream_index):
    ends = jnp.cumsum(seq_lengths)
    starts = ends - seq_lengths
    passed = (stream_index[:, None] >= ends[None, :]).astype(jnp.int32)
    sequence = jnp.sum(passed, axis=1)
    owner = sequence[:, None] == jnp.arange(seq_lengths.shape[0], dtype=jnp.int32)[None, :]
    opening = jnp.sum(jnp.where(owner, starts[None, :], 0), axis=1)
    return (sequence, stream_index - opening)


def slot_ranks(routes, ordering, experts):
    flat_routes = routes.reshape(-1)
    flat_order = ordering.reshape(-1)
    onehot = (flat_routes[:, None] == jnp.arange(experts, dtype=jnp.int32)[None, :]).astype(
        jnp.int32
    )
    arranged = jnp.zeros_like(onehot).at[flat_order].set(onehot)
    before = jnp.cumsum(arranged, axis=0) - arranged
    ranking = jnp.sum(before[flat_order] * onehot, axis=1)
    return ranking.reshape(routes.shape)


def scores_of(queries, keys, head_size):
    heads = queries.shape[1] // head_size
    query_heads = queries.reshape(queries.shape[0], heads, head_size)
    key_heads = keys.reshape(keys.shape[0], heads, head_size)
    return jnp.einsum(
        "qhd,khd->hqk", query_heads, key_heads, preferred_element_type=jnp.float32
    ) * (1.0 / math.sqrt(head_size))


def allowed_pairs(query_index, query_seq, key_index, key_seq):
    return (query_seq[:, None] == key_seq[None, :]) & (key_index[None, :] <= query_index[:, None])


def any_allowed(query_index, query_seq, key_index, key_seq):
    early = jnp.min(key_index) <= jnp.max(query_index)
    above = jnp.max(key_seq) >= jnp.min(query_seq)
    below = jnp.min(key_seq) <= jnp.max(query_seq)
    return early & above & below


def pair_forward(head_size, operands):
    queries, keys, values, query_index, query_seq, key_index, key_seq = operands
    scores = scores_of(queries, keys, head_size)
    allowed = allowed_pairs(query_index, query_seq, key_index, key_seq)
    expo = jnp.where(allowed[None], jnp.exp(scores), 0.0)
    heads = scores.shape[0]
    value_heads = values.reshape(values.shape[0], heads, head_size)
    summed = jnp.einsum(
        "hqk,khd->qhd", expo.astype(jnp.bfloat16), value_heads, preferred_element_type=jnp.float32
    )
    return (summed.reshape(queries.shape[0], queries.shape[1]), jnp.sum(expo, axis=-1))


def pair_forward_skip(head_size, operands):
    queries = operands[0]
    heads = queries.shape[1] // head_size
    return (
        jnp.zeros(queries.shape, jnp.float32),
        jnp.zeros((heads, queries.shape[0]), jnp.float32),
    )


def pair_backward(head_size, operands):
    queries, keys, values, scaled_grad, correction, query_index, query_seq, key_index, key_seq = (
        operands
    )
    scores = scores_of(queries, keys, head_size)
    allowed = allowed_pairs(query_index, query_seq, key_index, key_seq)
    expo = jnp.where(allowed[None], jnp.exp(scores), 0.0)
    heads = scores.shape[0]
    query_count = queries.shape[0]
    key_count = keys.shape[0]
    query_heads = queries.reshape(query_count, heads, head_size)
    key_heads = keys.reshape(key_count, heads, head_size)
    value_heads = values.reshape(key_count, heads, head_size)
    grad_heads = scaled_grad.reshape(query_count, heads, head_size)
    prob_grad = jnp.einsum(
        "qhd,khd->hqk", grad_heads, value_heads, preferred_element_type=jnp.float32
    )
    score_grad = (expo * (prob_grad - correction[:, :, None])).astype(jnp.bfloat16)
    factor = 1.0 / math.sqrt(head_size)
    query_part = (
        jnp.einsum("hqk,khd->qhd", score_grad, key_heads, preferred_element_type=jnp.float32)
        * factor
    )
    key_part = (
        jnp.einsum("hqk,qhd->khd", score_grad, query_heads, preferred_element_type=jnp.float32)
        * factor
    )
    value_part = jnp.einsum(
        "hqk,qhd->khd", expo.astype(jnp.bfloat16), grad_heads, preferred_element_type=jnp.float32
    )
    return (
        query_part.reshape(queries.shape),
        key_part.reshape(keys.shape),
        value_part.reshape(keys.shape),
    )


def pair_backward_skip(head_size, operands):
    queries = operands[0]
    keys = operands[1]
    return (
        jnp.zeros(queries.shape, jnp.float32),
        jnp.zeros(keys.shape, jnp.float32),
        jnp.zeros(keys.shape, jnp.float32),
    )


def attend_forward(queries, keys, values, query_index, query_seq, key_index, key_seq, head_size):
    rows, columns = queries.shape
    heads = columns // head_size
    half_rows = rows // 2
    groups = keys.shape[0] // rows
    query_blocks = queries.reshape(2, half_rows, columns)
    query_marks = query_index.reshape(2, half_rows)
    query_seqs = query_seq.reshape(2, half_rows)
    key_stack = (
        keys.reshape(groups, 2, half_rows, columns),
        values.reshape(groups, 2, half_rows, columns),
        key_index.reshape(groups, 2, half_rows),
        key_seq.reshape(groups, 2, half_rows),
    )

    def visit(carry, group):
        sums, totals = carry
        group_keys, group_values, group_index, group_seq = group
        sum_list = []
        total_list = []
        for query_part in range(2):
            running = sums[query_part]
            counted = totals[query_part]
            for key_part in range(2):
                operands = (
                    query_blocks[query_part],
                    group_keys[key_part],
                    group_values[key_part],
                    query_marks[query_part],
                    query_seqs[query_part],
                    group_index[key_part],
                    group_seq[key_part],
                )
                living = any_allowed(
                    query_marks[query_part],
                    query_seqs[query_part],
                    group_index[key_part],
                    group_seq[key_part],
                )
                add_sum, add_total = lax.cond(
                    living,
                    partial(pair_forward, head_size),
                    partial(pair_forward_skip, head_size),
                    operands,
                )
                running = running + add_sum
                counted = counted + add_total
            sum_list.append(running)
            total_list.append(counted)
        return ((jnp.stack(sum_list), jnp.stack(total_list)), None)

    initial = (
        jnp.zeros((2, half_rows, columns), jnp.float32),
        jnp.zeros((2, heads, half_rows), jnp.float32),
    )
    (sums, totals), unused = lax.scan(visit, initial, key_stack)
    totals_rows = jnp.transpose(totals, (1, 0, 2)).reshape(heads, rows)
    attended = sums.reshape(rows, heads, head_size) / jnp.transpose(totals_rows)[:, :, None]
    return (attended.reshape(rows, columns), totals_rows)


def attend_backward(
    queries,
    keys,
    values,
    scaled_grad,
    correction,
    query_index,
    query_seq,
    key_index,
    key_seq,
    head_size,
):
    rows, columns = queries.shape
    heads = columns // head_size
    half_rows = rows // 2
    groups = keys.shape[0] // rows
    query_blocks = queries.reshape(2, half_rows, columns)
    scaled_blocks = scaled_grad.reshape(2, half_rows, columns)
    correction_blocks = jnp.transpose(correction.reshape(heads, 2, half_rows), (1, 0, 2))
    query_marks = query_index.reshape(2, half_rows)
    query_seqs = query_seq.reshape(2, half_rows)
    key_stack = (
        keys.reshape(groups, 2, half_rows, columns),
        values.reshape(groups, 2, half_rows, columns),
        key_index.reshape(groups, 2, half_rows),
        key_seq.reshape(groups, 2, half_rows),
    )

    def visit(carry, group):
        group_keys, group_values, group_index, group_seq = group
        key_list = [
            jnp.zeros((half_rows, columns), jnp.float32),
            jnp.zeros((half_rows, columns), jnp.float32),
        ]
        value_list = [
            jnp.zeros((half_rows, columns), jnp.float32),
            jnp.zeros((half_rows, columns), jnp.float32),
        ]
        query_list = []
        for query_part in range(2):
            running = carry[query_part]
            for key_part in range(2):
                operands = (
                    query_blocks[query_part],
                    group_keys[key_part],
                    group_values[key_part],
                    scaled_blocks[query_part],
                    correction_blocks[query_part],
                    query_marks[query_part],
                    query_seqs[query_part],
                    group_index[key_part],
                    group_seq[key_part],
                )
                living = any_allowed(
                    query_marks[query_part],
                    query_seqs[query_part],
                    group_index[key_part],
                    group_seq[key_part],
                )
                add_query, add_key, add_value = lax.cond(
                    living,
                    partial(pair_backward, head_size),
                    partial(pair_backward_skip, head_size),
                    operands,
                )
                running = running + add_query
                key_list[key_part] = key_list[key_part] + add_key
                value_list[key_part] = value_list[key_part] + add_value
            query_list.append(running)
        return (jnp.stack(query_list), (jnp.stack(key_list), jnp.stack(value_list)))

    query_grad, (key_grads, value_grads) = lax.scan(
        visit, jnp.zeros((2, half_rows, columns), jnp.float32), key_stack
    )
    return (
        query_grad.reshape(rows, columns),
        key_grads.reshape(groups * rows, columns),
        value_grads.reshape(groups * rows, columns),
    )


def gather_keys(key_rows, value_rows):
    return (
        lax.all_gather(key_rows, "blk", axis=0, tiled=True),
        lax.all_gather(value_rows, "blk", axis=0, tiled=True),
    )


def gather_experts(gate_rows, up_rows, down_rows):
    return (
        lax.all_gather(gate_rows, "head", axis=1, tiled=True),
        lax.all_gather(up_rows, "head", axis=1, tiled=True),
        lax.all_gather(down_rows, "head", axis=1, tiled=True),
    )


def on_device(
    tokens,
    query_weight,
    key_weight,
    value_weight,
    output_weight,
    mixing_gain,
    query_gain,
    key_gain,
    routing_gain,
    router_weight,
    gate_weight,
    up_weight,
    down_weight,
    seq_lengths,
    dealt_order,
    expert_routes,
    slot_order,
    cotangent,
):
    head_count = lax.axis_size("head")
    block_count = lax.axis_size("blk")
    head_at = lax.axis_index("head")
    block_at = lax.axis_index("blk")
    local_rows, width = tokens.shape
    picks = expert_routes.shape[1]
    total_rows = dealt_order.shape[0]
    group_rows = local_rows * head_count
    head_size = HDIM
    float_type = jnp.float32
    half_type = jnp.bfloat16
    gathered = (
        lax.all_gather(query_weight, ("head", "blk"), axis=0, tiled=True),
        lax.all_gather(key_weight, ("head", "blk"), axis=0, tiled=True),
        lax.all_gather(value_weight, ("head", "blk"), axis=0, tiled=True),
        lax.all_gather(output_weight, ("head", "blk"), axis=0, tiled=True),
        lax.all_gather(router_weight, ("head", "blk"), axis=0, tiled=True),
        lax.all_gather(mixing_gain, ("head", "blk"), axis=0, tiled=True),
        lax.all_gather(query_gain, ("head", "blk"), axis=0, tiled=True),
        lax.all_gather(key_gain, ("head", "blk"), axis=0, tiled=True),
        lax.all_gather(routing_gain, ("head", "blk"), axis=0, tiled=True),
    )
    query_full, key_full, value_full, output_full, router_full = (
        gathered[0],
        gathered[1],
        gathered[2],
        gathered[3],
        gathered[4],
    )
    mixing_scale = gathered[5].astype(float_type)
    query_scale = gathered[6].astype(float_type)
    key_scale = gathered[7].astype(float_type)
    routing_scale = gathered[8].astype(float_type)
    experts = router_full.shape[1]
    local_experts = gate_weight.shape[0]
    capacity = 5 * local_rows * picks // (4 * experts)
    heads_here = query_full.shape[1] // head_size // head_count
    own_block = head_at * block_count + block_at
    own_index = lax.dynamic_slice_in_dim(dealt_order, own_block * local_rows, local_rows)
    own_position = stream_layout(seq_lengths, own_index)[1]
    key_index = jnp.transpose(
        dealt_order.reshape(head_count, block_count, local_rows), (1, 0, 2)
    ).reshape(total_rows)
    key_seq = stream_layout(seq_lengths, key_index)[0]
    query_index = lax.dynamic_slice_in_dim(key_index, block_at * group_rows, group_rows)
    query_seq = lax.dynamic_slice_in_dim(key_seq, block_at * group_rows, group_rows)
    tokens_float = tokens.astype(float_type)
    normed = rmsnorm(tokens_float, mixing_scale).astype(half_type)
    query_raw = jnp.dot(normed, query_full, preferred_element_type=float_type)
    key_raw = jnp.dot(normed, key_full, preferred_element_type=float_type)
    query_rows = norm_rotate(query_raw, query_scale, own_position, head_size).astype(half_type)
    key_rows = norm_rotate(key_raw, key_scale, own_position, head_size).astype(half_type)
    value_rows = jnp.dot(normed, value_full, preferred_element_type=float_type).astype(half_type)
    query_heads, key_heads, value_heads = (
        lax.all_to_all(query_rows, "head", split_axis=1, concat_axis=0, tiled=True),
        lax.all_to_all(key_rows, "head", split_axis=1, concat_axis=0, tiled=True),
        lax.all_to_all(value_rows, "head", split_axis=1, concat_axis=0, tiled=True),
    )
    keys_all, values_all = gather_keys(key_heads, value_heads)
    attended, totals = attend_forward(
        query_heads, keys_all, values_all, query_index, query_seq, key_index, key_seq, head_size
    )
    context_cols = attended.astype(half_type)
    context = lax.all_to_all(context_cols, "head", split_axis=0, concat_axis=1, tiled=True)
    middle = tokens_float + jnp.dot(context, output_full, preferred_element_type=float_type)
    routed = rmsnorm(middle, routing_scale).astype(half_type)
    probs = jax.nn.softmax(jnp.dot(routed, router_full, preferred_element_type=float_type), axis=-1)
    expert_ids = jnp.arange(experts, dtype=jnp.int32)
    chosen = expert_routes[:, :, None] == expert_ids[None, None, :]
    weights = jnp.sum(jnp.where(chosen, probs[:, None, :], 0.0), axis=2)
    ranking = slot_ranks(expert_routes, slot_order, experts)
    is_kept = ranking < capacity
    per_source = block_count * capacity
    slots = jnp.where(
        is_kept,
        expert_routes % local_experts * per_source
        + expert_routes // local_experts * capacity
        + ranking,
        local_experts * per_source,
    )
    slot_list = slots.reshape(-1)
    outgoing = (
        jnp.zeros((local_experts * per_source, width), half_type)
        .at[slot_list]
        .set(jnp.repeat(routed, picks, axis=0), mode="drop")
    )
    arrived = lax.all_to_all(
        outgoing.reshape(local_experts, per_source, width),
        "blk",
        split_axis=1,
        concat_axis=1,
        tiled=True,
    )
    gate_all, up_all, down_all = gather_experts(gate_weight, up_weight, down_weight)
    gate = jnp.einsum("esd,edf->esf", arrived, gate_all, preferred_element_type=float_type)
    upward = jnp.einsum("esd,edf->esf", arrived, up_all, preferred_element_type=float_type)
    active = (jax.nn.silu(gate) * upward).astype(half_type)
    produced = jnp.einsum(
        "esf,efd->esd", active, down_all, preferred_element_type=float_type
    ).astype(half_type)
    returned = lax.all_to_all(produced, "blk", split_axis=1, concat_axis=1, tiled=True).reshape(
        local_experts * per_source, width
    )
    pair_out = jnp.take(returned, slots, axis=0, mode="fill", fill_value=0)
    combined = jnp.sum(weights[:, :, None] * pair_out, axis=1)
    block_output = (middle + combined).astype(half_type)
    upstream = cotangent.astype(float_type)
    pair_grad = jnp.where(
        is_kept[:, :, None], weights[:, :, None] * upstream[:, None, :], 0.0
    ).astype(half_type)
    weight_grad = jnp.sum(upstream[:, None, :] * pair_out, axis=2)
    prob_grad = jnp.sum(jnp.where(chosen, weight_grad[:, :, None], 0.0), axis=1)
    logit_grad = (probs * (prob_grad - jnp.sum(probs * prob_grad, axis=1, keepdims=True))).astype(
        half_type
    )
    router_sum = jnp.dot(routed.T, logit_grad, preferred_element_type=float_type)
    routed_grad = jnp.dot(logit_grad, router_full.T, preferred_element_type=float_type)
    pair_buffer = (
        jnp.zeros((local_experts * per_source, width), half_type)
        .at[slot_list]
        .set(pair_grad.reshape(-1, width), mode="drop")
    )
    arrived_grad = lax.all_to_all(
        pair_buffer.reshape(local_experts, per_source, width),
        "blk",
        split_axis=1,
        concat_axis=1,
        tiled=True,
    )
    gate_again, up_again, down_again, arrived_grad = lax.optimization_barrier(
        (gate_weight, up_weight, down_weight, arrived_grad)
    )
    gate_all, up_all, down_all = gather_experts(gate_again, up_again, down_again)
    active_grad = jnp.einsum(
        "esd,efd->esf", arrived_grad, down_all, preferred_element_type=float_type
    )
    down_sum = jnp.einsum("esf,esd->efd", active, arrived_grad, preferred_element_type=float_type)
    unused, gating_back = jax.vjp(
        lambda gate_in, upward_in: jax.nn.silu(gate_in) * upward_in, gate, upward
    )
    gate_grad, upward_grad = gating_back(active_grad)
    gate_grad = gate_grad.astype(half_type)
    upward_grad = upward_grad.astype(half_type)
    gate_sum = jnp.einsum("esd,esf->edf", arrived, gate_grad, preferred_element_type=float_type)
    up_sum = jnp.einsum("esd,esf->edf", arrived, upward_grad, preferred_element_type=float_type)
    incoming_grad = jnp.einsum(
        "esf,edf->esd", gate_grad, gate_all, preferred_element_type=float_type
    )
    incoming_grad = (
        incoming_grad
        + jnp.einsum("esf,edf->esd", upward_grad, up_all, preferred_element_type=float_type)
    ).astype(half_type)
    gate_shard, up_shard, down_shard = (
        lax.psum_scatter(
            gate_sum.astype(jnp.bfloat16), "head", scatter_dimension=1, tiled=True
        ).astype(jnp.float32),
        lax.psum_scatter(
            up_sum.astype(jnp.bfloat16), "head", scatter_dimension=1, tiled=True
        ).astype(jnp.float32),
        lax.psum_scatter(
            down_sum.astype(jnp.bfloat16), "head", scatter_dimension=1, tiled=True
        ).astype(jnp.float32),
    )
    back_rows = lax.all_to_all(
        incoming_grad, "blk", split_axis=1, concat_axis=1, tiled=True
    ).reshape(local_experts * per_source, width)
    routed_grad = routed_grad + jnp.sum(
        jnp.take(back_rows, slots, axis=0, mode="fill", fill_value=0), axis=1, dtype=float_type
    )
    unused, routing_back = jax.vjp(rmsnorm, middle, routing_scale)
    middle_add, routing_sum = routing_back(routed_grad)
    middle_grad = upstream + middle_add
    branch_grad = middle_grad.astype(half_type)
    context_grad = jnp.dot(branch_grad, output_full.T, preferred_element_type=float_type).astype(
        half_type
    )
    context_heads = lax.all_to_all(context_grad, "head", split_axis=1, concat_axis=0, tiled=True)
    key_again, value_again, context_heads = lax.optimization_barrier(
        (key_heads, value_heads, context_heads)
    )
    keys_all, values_all = gather_keys(key_again, value_again)
    context_float = context_heads.astype(float_type).reshape(group_rows, heads_here, head_size)
    scaled_grad = (
        (context_float / jnp.transpose(totals)[:, :, None])
        .astype(half_type)
        .reshape(group_rows, heads_here * head_size)
    )
    correction = (
        jnp.transpose(
            jnp.sum(context_float * attended.reshape(group_rows, heads_here, head_size), axis=2)
        )
        / totals
    )
    query_grad_heads, key_grad_all, value_grad_all = attend_backward(
        query_heads,
        keys_all,
        values_all,
        scaled_grad,
        correction,
        query_index,
        query_seq,
        key_index,
        key_seq,
        head_size,
    )
    key_grad_own, value_grad_own = (
        lax.psum_scatter(
            key_grad_all.astype(jnp.bfloat16), "blk", scatter_dimension=0, tiled=True
        ).astype(jnp.float32),
        lax.psum_scatter(
            value_grad_all.astype(jnp.bfloat16), "blk", scatter_dimension=0, tiled=True
        ).astype(jnp.float32),
    )
    value_cols = value_grad_own.astype(half_type)
    query_back, key_back, value_back = (
        lax.all_to_all(
            as_sent(query_grad_heads.astype(half_type)),
            "head",
            split_axis=0,
            concat_axis=1,
            tiled=True,
        ),
        lax.all_to_all(
            as_sent(key_grad_own.astype(half_type)), "head", split_axis=0, concat_axis=1, tiled=True
        ),
        lax.all_to_all(as_sent(value_cols), "head", split_axis=0, concat_axis=1, tiled=True).astype(
            value_cols.dtype
        ),
    )
    unused, query_turn_back = jax.vjp(
        lambda raw, gain: norm_rotate(raw, gain, own_position, head_size), query_raw, query_scale
    )
    query_raw_grad, querynorm_sum = query_turn_back(query_back.astype(float_type))
    unused, key_turn_back = jax.vjp(
        lambda raw, gain: norm_rotate(raw, gain, own_position, head_size), key_raw, key_scale
    )
    key_raw_grad, keynorm_sum = key_turn_back(key_back.astype(float_type))
    query_raw_grad = query_raw_grad.astype(half_type)
    key_raw_grad = key_raw_grad.astype(half_type)
    normed_grad = jnp.dot(query_raw_grad, query_full.T, preferred_element_type=float_type)
    normed_grad = normed_grad + jnp.dot(key_raw_grad, key_full.T, preferred_element_type=float_type)
    normed_grad = normed_grad + jnp.dot(value_back, value_full.T, preferred_element_type=float_type)
    unused, mixing_back = jax.vjp(rmsnorm, tokens_float, mixing_scale)
    token_add, mixing_sum = mixing_back(normed_grad)
    tokens_grad = middle_grad + token_add
    query_sum = jnp.dot(normed.T, query_raw_grad, preferred_element_type=float_type)
    key_sum = jnp.dot(normed.T, key_raw_grad, preferred_element_type=float_type)
    value_sum = jnp.dot(normed.T, value_back, preferred_element_type=float_type)
    output_sum = jnp.dot(context.T, branch_grad, preferred_element_type=float_type)
    summed = (
        lax.psum_scatter(query_sum, ("head", "blk"), scatter_dimension=0, tiled=True),
        lax.psum_scatter(key_sum, ("head", "blk"), scatter_dimension=0, tiled=True),
        lax.psum_scatter(value_sum, ("head", "blk"), scatter_dimension=0, tiled=True),
        lax.psum_scatter(output_sum, ("head", "blk"), scatter_dimension=0, tiled=True),
        lax.psum_scatter(router_sum, ("head", "blk"), scatter_dimension=0, tiled=True),
        lax.psum_scatter(mixing_sum, ("head", "blk"), scatter_dimension=0, tiled=True),
        lax.psum_scatter(querynorm_sum, ("head", "blk"), scatter_dimension=0, tiled=True),
        lax.psum_scatter(keynorm_sum, ("head", "blk"), scatter_dimension=0, tiled=True),
        lax.psum_scatter(routing_sum, ("head", "blk"), scatter_dimension=0, tiled=True),
    )
    query_out, key_out, value_out, output_out = (summed[0], summed[1], summed[2], summed[3])
    router_out, mixing_out, querynorm_out, keynorm_out, routing_out = (
        summed[4],
        summed[5],
        summed[6],
        summed[7],
        summed[8],
    )
    return (
        block_output,
        tokens_grad,
        query_out,
        key_out,
        value_out,
        output_out,
        mixing_out,
        querynorm_out,
        keynorm_out,
        routing_out,
        router_out,
        gate_shard,
        up_shard,
        down_shard,
    )


def solution(mesh):
    in_specs = (
        P(("head", "blk"), None),
        P(("head", "blk"), None),
        P(("head", "blk"), None),
        P(("head", "blk"), None),
        P(("head", "blk"), None),
        P(("head", "blk")),
        P(("head", "blk")),
        P(("head", "blk")),
        P(("head", "blk")),
        P(("head", "blk"), None),
        P("blk", "head", None),
        P("blk", "head", None),
        P("blk", "head", None),
        P(),
        P(),
        P(("head", "blk"), None),
        P(("head", "blk"), None),
        P(("head", "blk"), None),
    )
    out_specs = (
        P(("head", "blk"), None),
        P(("head", "blk"), None),
        P(("head", "blk"), None),
        P(("head", "blk"), None),
        P(("head", "blk"), None),
        P(("head", "blk"), None),
        P(("head", "blk")),
        P(("head", "blk")),
        P(("head", "blk")),
        P(("head", "blk")),
        P(("head", "blk"), None),
        P("blk", "head", None),
        P("blk", "head", None),
        P("blk", "head", None),
    )
    return jax.shard_map(
        on_device, mesh=mesh, in_specs=in_specs, out_specs=out_specs, check_vma=False
    )
```

profile of v0, /device:TPU:0, one launch (start us, length us, event | category | flops | bytes accessed | tf_op | source)
XLA Modules:
  0.0 3037.6 jit_solution(452061554762323326)
XLA Ops:
  12.9 42.9 %all-reduce.13 = (bf16[2048]{0:T(1024)(128)(2,1)S(1)}, bf16[2048]{0:T(1024)(128)(2,1)S(1)}, bf16[2048]{0:T(1024)(128)(2,1)S(1)}, bf16[2048]{0:T(1024)(128)(2,1)S(1)}) all-reduce(bf16[2048]{0:T(1024)(128)(2,1)S(1)} %dynamic-update-slice, bf16[2048]{0:T(1024)(128)(2,1)S(1)} %dynamic-update-slice.1, ...), channel_id=1, replica_groups=mesh['head'=4,'blk'=8] {'head','blk'}, use_global_device_ids=true, to_apply=%add.4 | all-reduce | flops 8192 | bytes 32768
  61.1 30.0 all-gather.16.cloned.1.call-done
  97.5 72.3 %all-gather.18.cloned.1.call-done = bf16[2048,2048]{1,0:T(8,128)(2,1)} async-done(((bf16[64,2048]{1,0:T(8,128)(2,1)}), bf16[2048,2048]{1,0:T(8,128)(2,1)}) %all-gather.18.cloned.1.call-update) | async-done | bytes 8388624 | tf_op jit(solution)/shard_map/all_gather | solution.py:350
  178.6 12.2 all_to_all.145
  191.9 59.9 %all-gather.22.cloned.1.call-done = bf16[2048,2048]{1,0:T(8,128)(2,1)} async-done(((bf16[64,2048]{1,0:T(8,128)(2,1)}), bf16[2048,2048]{1,0:T(8,128)(2,1)}) %all-gather.22.cloned.1.call-update) | async-done | bytes 8388624 | tf_op jit(solution)/shard_map/all_gather | solution.py:351
  256.5 12.3 all_to_all.146
  289.6 42.8 %all-gather = bf16[32,64,16]{1,2,0:T(8,128)(2,1)S(1)} all-gather(bf16[1,64,16]{1,2,0:T(8,128)(2,1)S(1)} %bitcast.532), channel_id=1, replica_groups=mesh['head'=4,'blk'=8] {'head','blk'}, dimensions={0}, use_global_device_ids=true | all-gather | bytes 67584 | tf_op jit(solution)/shard_map/all_gather | solution.py:353
  336.3 10.9 all-gather.24.cloned.1.call-done
  348.2 207.7 %while.28 = (s32[]{:T(128)}, f32[2,256,512]{1,2,0:T(8,128)}, f32[2,4,256]{2,1,0:T(4,128)S(1)}, s32[8,2,256]{2,1,0:T(2,128)}, s32[]{:T(128)}, /*index=5*/s32[8,2,...) while((s32[]{:T(128)}, f32[2,256,512]{1,2,0:T(8,128)}, ...), condition=%wide.region_32.33_spmd, body=%wide.region_13.32_spmd.sunk | while | flops 542641664 | bytes 24740512 | solution.py:215
  565.9 13.5 all-to-all-done.3
  587.3 18.4 scatter_custom_fusion.2
  605.7 10.2 copy.595
  615.9 121.0 %all_to_all.147 = bf16[2,640,2048]{2,0,1:T(2,128)(2,1)} all-to-all(bf16[2,640,2048]{2,0,1:T(2,128)(2,1)} %copy.595), channel_id=1, replica_groups=mesh['head'=4,'blk'=8] {'blk'}, dimensions={1} | all-to-all | bytes 10485760 | tf_op jit(solution)/shard_map/all_to_all | solution.py:459
  748.4 10.2 copy.588
  763.9 115.9 %all-to-all-done.4 = bf16[2,640,2048]{2,0,1:T(2,128)(2,1)} async-done(((bf16[2,640,2048]{2,0,1:T(2,128)(2,1)}), bf16[2,640,2048]{2,0,1:T(2,128)(2,1)}, u32[]{:S(2)}, u32[]{:S(2)}) %all-to-all-start.4) | async-done | bytes 5242912 | tf_op jit(solution)/shard_map/all_to_all | solution.py:423
  879.8 13.8 copy.614
  893.6 11.2 fusion.164
  904.8 11.2 fusion.165
  915.9 19.2 multiply_convert_fusion
  935.1 12.4 fusion.166
  947.5 53.6 %all-gather.38.cloned.1.call-done = bf16[2,2048,1024]{2,1,0:T(8,128)(2,1)} async-done(((bf16[2,512,1024]{2,1,0:T(8,128)(2,1)}), bf16[2,2048,1024]{2,1,0:T(8,128)(2,1)}) %all-gather.38.cloned.1.call-update) | async-done | bytes 8388624 | tf_op jit(solution)/shard_map/all_gather | solution.py:312
  1001.1 12.6 add_convert_fusion
  1013.7 10.5 copy.597
  1029.4 60.8 %all-gather.32.cloned.1.call-done = bf16[2,1024,2048]{2,1,0:T(8,128)(2,1)} async-done(((bf16[2,256,2048]{2,1,0:T(8,128)(2,1)}), bf16[2,1024,2048]{2,1,0:T(8,128)(2,1)}) %all-gather.32.cloned.1.call-update) | async-done | bytes 8388624 | tf_op jit(solution)/shard_map/all_gather | solution.py:313
  1090.3 11.0 convolution_convert_fusion.3
  1101.3 10.2 copy.591
  1111.5 34.4 %all-to-all-done.7 = bf16[2,640,2048]{2,0,1:T(2,128)(2,1)} async-done(((bf16[2,640,2048]{2,0,1:T(2,128)(2,1)}), bf16[2,640,2048]{2,0,1:T(2,128)(2,1)}, u32[]{:S(2)}, u32[]{:S(2)}) %all-to-all-start.7) | async-done | bytes 5242912 | tf_op jit(solution)/shard_map/all_to_all | solution.py:500
  1158.1 12.1 gather_fusion.2
  1170.2 96.8 %all-to-all-done.5 = bf16[2,640,2048]{2,0,1:T(2,128)(2,1)} async-done(((bf16[2,640,2048]{2,0,1:T(2,128)(2,1)}), bf16[2,640,2048]{2,0,1:T(2,128)(2,1)}, u32[]{:S(2)}, u32[]{:S(2)}) %all-to-all-start.5) | async-done | bytes 5242912 | tf_op jit(solution)/shard_map/all_to_all | solution.py:437
  1274.2 12.0 gather_fusion.1
  1286.2 11.9 fusion.85
  1309.8 11.2 all_to_all.148
  1331.4 34.5 %all-gather.40.cloned.1.call-done = bf16[4096,512]{1,0:T(8,128)(2,1)} async-done(((bf16[512,512]{1,0:T(8,128)(2,1)}), bf16[4096,512]{1,0:T(8,128)(2,1)}) %all-gather.40.cloned.1.call-update) | async-done | bytes 4194320 | tf_op jit(solution)/shard_map/all_gather | solution.py:304
  1365.9 47.2 %all-gather.42.cloned.1.call-done = bf16[4096,512]{1,0:T(8,128)(2,1)} async-done(((bf16[512,512]{1,0:T(8,128)(2,1)}), bf16[4096,512]{1,0:T(8,128)(2,1)}) %all-gather.42.cloned.1.call-update) | async-done | bytes 4194320 | tf_op jit(solution)/shard_map/all_gather | solution.py:305
  1414.1 362.6 %while.29 = (s32[]{:T(128)}, f32[2,256,512]{1,2,0:T(8,128)}, bf16[8,2,256,512]{3,2,1,0:T(8,128)(2,1)}, bf16[8,2,256,512]{3,2,1,0:T(8,128)(2,1)}, s32[8,2,256]{2,...) while((s32[]{:T(128)}, f32[2,256,512]{1,2,0:T(8,128)}, ...), condition=%wide.region_65.67_spmd, body=%wide.region_50.66_spmd.sunk | while | flops 1352664576 | bytes 63505748 | solution.py:292
  1779.2 14.2 convolution_convert_fusion
  1795.1 11.6 convolution_convert_fusion.2
  1808.5 11.5 convolution_convert_fusion.1
  1830.8 10.3 all_to_all.149
  1906.9 107.2 %reduce-scatter.31.cloned.1.call-done = f32[64,16]{1,0:T(8,128)} async-done(((f32[2048,16]{1,0:T(8,128)}), f32[64,16]{1,0:T(8,128)}) %reduce-scatter.31.cloned.1.call-update) | async-done | bytes 4112
  2015.5 84.3 %reduce-scatter.29.cloned.1.call-done = bf16[2,256,2048]{2,1,0:T(8,128)(2,1)} async-done(((bf16[2,1024,2048]{2,1,0:T(8,128)(2,1)}), bf16[2,256,2048]{2,1,0:T(8,128)(2,1)}) %reduce-scatter.29.cloned.1.call-update) | async-done | bytes 2097168 | tf_op jit(solution)/shard_map/reduce_scatter | solution.py:496
  2103.9 85.3 %reduce-scatter.25.cloned.1.call-done = bf16[2,512,1024]{2,1,0:T(8,128)(2,1)} async-done(((bf16[2,2048,1024]{2,1,0:T(8,128)(2,1)}), bf16[2,512,1024]{2,1,0:T(8,128)(2,1)}) %reduce-scatter.25.cloned.1.call-update) | async-done | bytes 2097168 | tf_op jit(solution)/shard_map/reduce_scatter | solution.py:490
  2193.3 85.2 %reduce-scatter.27.cloned.1.call-done = bf16[2,512,1024]{2,1,0:T(8,128)(2,1)} async-done(((bf16[2,2048,1024]{2,1,0:T(8,128)(2,1)}), bf16[2,512,1024]{2,1,0:T(8,128)(2,1)}) %reduce-scatter.27.cloned.1.call-update) | async-done | bytes 2097168 | tf_op jit(solution)/shard_map/reduce_scatter | solution.py:493
  2296.2 41.6 %all-reduce.12 = (f32[2048]{0:T(1024)S(1)}, f32[2048]{0:T(1024)S(1)}, f32[2048]{0:T(1024)S(1)}, f32[2048]{0:T(1024)S(1)}) all-reduce(f32[2048]{0:T(1024)S(1)} %get-tuple-element.783, f32[2048]{0:T(1024)S(1)} %get-tuple-element.781, f32[2048]{0:T(1024)S(1)} %get-tuple-element.779, ...), channel_id=8, replica_groups=mesh['head'=4,'blk'=8] {'head','blk'}, use_global_device_ids=true, to_apply=%region_76.78.clone | all-reduce | flops 8192 | bytes 65536
  2342.6 126.4 %reduce-scatter.23.cloned.1.call-done = f32[64,2048]{1,0:T(8,128)} async-done(((f32[2048,2048]{1,0:T(8,128)}), f32[64,2048]{1,0:T(8,128)}) %reduce-scatter.23.cloned.1.call-update) | async-done | bytes 524304 | tf_op jit(solution)/shard_map/reduce_scatter | solution.py:590
  2469.0 187.2 %reduce-scatter.19.cloned.1.call-done = f32[64,2048]{1,0:T(8,128)} async-done(((f32[2048,2048]{1,0:T(8,128)}), f32[64,2048]{1,0:T(8,128)}) %reduce-scatter.19.cloned.1.call-update) | async-done | bytes 524304 | tf_op jit(solution)/shard_map/reduce_scatter | solution.py:588
  2656.2 187.2 %reduce-scatter.17.cloned.1.call-done = f32[64,2048]{1,0:T(8,128)} async-done(((f32[2048,2048]{1,0:T(8,128)}), f32[64,2048]{1,0:T(8,128)}) %reduce-scatter.17.cloned.1.call-update) | async-done | bytes 524304 | tf_op jit(solution)/shard_map/reduce_scatter | solution.py:587
  2843.4 187.1 %reduce-scatter.21.cloned.1.call-done = f32[64,2048]{1,0:T(8,128)} async-done(((f32[2048,2048]{1,0:T(8,128)}), f32[64,2048]{1,0:T(8,128)}) %reduce-scatter.21.cloned.1.call-update) | async-done | bytes 524304 | tf_op jit(solution)/shard_map/reduce_scatter | solution.py:589
  (943 shorter events, 691.0 us)
Async XLA Ops:
  7.2 83.9 %all-gather.16.cloned.1.call-start = ((), (), s32[]{:S(2)}) async-start(), calls=%async_computation.22 | async-start | bytes 8650752 | tf_op jit(solution)/shard_map/all_gather | solution.py:349
  7.9 161.9 %all-gather.18.cloned.1.call-start = ((), (), s32[]{:S(2)}) async-start(), calls=%async_computation.23 | async-start | bytes 8650752 | tf_op jit(solution)/shard_map/all_gather | solution.py:350
  8.7 243.1 %all-gather.22.cloned.1.call-start = ((), (), s32[]{:S(2)}) async-start(), calls=%async_computation.25 | async-start | bytes 8650752 | tf_op jit(solution)/shard_map/all_gather | solution.py:351
  9.4 326.9 %all-gather.20.cloned.1.call-start = ((), (), s32[]{:S(2)}) async-start(), calls=%async_computation.24 | async-start | bytes 4718592 | tf_op jit(solution)/shard_map/all_gather | solution.py:304
  55.8 196.0 %copy-start.23 = (f32[2048]{0:T(1024)}, f32[2048]{0:T(1024)S(1)}, u32[]{:S(2)}) copy-start(f32[2048]{0:T(1024)S(1)} %convert_element_type.238) | copy-start | bytes 24580
  55.8 40.3 %copy-start.43 = (f32[2048]{0:T(1024)}, f32[2048]{0:T(1024)S(1)}, u32[]{:S(2)}) copy-start(f32[2048]{0:T(1024)S(1)} %convert_element_type.240) | copy-start | bytes 24580
  55.8 118.8 %copy-start.45 = (f32[2048]{0:T(1024)}, f32[2048]{0:T(1024)S(1)}, u32[]{:S(2)}) copy-start(f32[2048]{0:T(1024)S(1)} %convert_element_type.244) | copy-start | bytes 24580
  60.1 191.7 %copy-start.47 = (f32[128]{0:T(128)}, f32[128]{0:T(128)S(1)}, u32[]{:S(2)}) copy-start(f32[128]{0:T(128)S(1)} %fusion.135) | copy-start | bytes 1540
  61.0 117.2 %copy-start.35 = (f32[128,64]{0,1:T(8,128)}, f32[128,64]{0,1:T(8,128)S(1)}, u32[]{:S(2)}) copy-start(f32[128,64]{0,1:T(8,128)S(1)} %get-tuple-element.953) | copy-start | bytes 98308
  61.0 117.2 %copy-start.37 = (f32[128,64]{0,1:T(8,128)}, f32[128,64]{0,1:T(8,128)S(1)}, u32[]{:S(2)}) copy-start(f32[128,64]{0,1:T(8,128)S(1)} %get-tuple-element.954) | copy-start | bytes 98308
  61.1 108.7 %copy-start = (bf16[128,2048]{1,0:T(8,128)(2,1)S(1)}, bf16[128,2048]{1,0:T(8,128)(2,1)}, u32[]{:S(2)}) copy-start(bf16[128,2048]{1,0:T(8,128)(2,1)} %param.40) | copy-start | bytes 1572868
  96.0 78.5 %copy-start.61 = (f32[128]{0:T(128)}, f32[128]{0:T(128)S(1)}, u32[]{:S(2)}) copy-start(f32[128]{0:T(128)S(1)} %get-tuple-element.957) | copy-start | bytes 1540
  96.1 78.5 %copy-start.53 = (f32[128]{0:T(128)}, f32[128]{0:T(128)S(1)}, u32[]{:S(2)}) copy-start(f32[128]{0:T(128)S(1)} %fusion.136) | copy-start | bytes 1540
  191.8 155.3 %all-gather.24.cloned.1.call-start = ((), (), s32[]{:S(2)}) async-start(), calls=%async_computation.26 | async-start | bytes 4718592 | tf_op jit(solution)/shard_map/all_gather | solution.py:305
  268.9 312.7 %all-gather.26.cloned.1.call-start = ((), (), s32[]{:S(2)}) async-start(), calls=%async_computation.27 | async-start | bytes 8650752 | tf_op jit(solution)/shard_map/all_gather | solution.py:352
  269.4 624.2 %all-gather.28.cloned.1.call-start = ((), (), s32[]{:S(2)}) async-start(), calls=%async_computation.28 | async-start | bytes 10485760 | tf_op jit(solution)/shard_map/all_gather | solution.py:311
  270.2 634.6 %all-gather.30.cloned.1.call-start = ((), (), s32[]{:S(2)}) async-start(), calls=%async_computation.29 | async-start | bytes 10485760 | tf_op jit(solution)/shard_map/all_gather | solution.py:312
  280.3 53.2 %copy-start.27 = (bf16[128,2048]{1,0:T(8,128)(2,1)S(1)}, bf16[128,2048]{1,0:T(8,128)(2,1)}, u32[]{:S(2)}) copy-start(bf16[128,2048]{1,0:T(8,128)(2,1)} %param.57) | copy-start | bytes 1572868
  284.6 50.7 %all-to-all-start = ((bf16[128,4,512]{0,2,1:T(8,128)(2,1)}), bf16[128,4,512]{0,2,1:T(8,128)(2,1)S(1)}, u32[]{:S(2)}, u32[]{:S(2)}) async-start(bf16[128,4,512]{0,2,1:T(8,128)(2,1)} %bitcast.124), calls=%async_computation | async-start | bytes 1048576 | tf_op jit(solution)/shard_map/all_to_all | solution.py:391
  555.9 25.6 copy-start.33
  555.9 25.7 copy-start.39
  555.9 25.7 copy-start.41
  562.2 17.2 all-to-all-start.3
  565.9 350.0 %all-gather.34.cloned.1.call-start = ((), (), s32[]{:S(2)}) async-start(), calls=%async_computation.31 | async-start | bytes 10485760 | tf_op jit(solution)/shard_map/all_gather | solution.py:313
  586.7 151.5 %copy-start.17 = (bf16[128,2048]{1,0:T(8,128)(2,1)}, bf16[128,2048]{1,0:T(8,128)(2,1)S(1)}, u32[]{:S(2)}) copy-start(bf16[128,2048]{1,0:T(8,128)(2,1)S(1)} %multiply_convert_fusion.2) | copy-start | bytes 1572868
  736.9 198.2 %all-gather.36.cloned.1.call-start = ((), (), s32[]{:S(2)}) async-start(), calls=%async_computation.32 | async-start | bytes 10485760 | tf_op jit(solution)/shard_map/all_gather | solution.py:311
  737.5 263.6 %all-gather.38.cloned.1.call-start = ((), (), s32[]{:S(2)}) async-start(), calls=%async_computation.33 | async-start | bytes 10485760 | tf_op jit(solution)/shard_map/all_gather | solution.py:312
  758.6 121.2 %all-to-all-start.4 = ((bf16[2,640,2048]{2,0,1:T(2,128)(2,1)}), bf16[2,640,2048]{2,0,1:T(2,128)(2,1)}, u32[]{:S(2)}, u32[]{:S(2)}) async-start(bf16[2,640,2048]{2,0,1:T(2,128)(2,1)} %copy.588), calls=%async_computation.4 | async-start | bytes 10485760 | tf_op jit(solution)/shard_map/all_to_all | solution.py:423
  763.3 326.9 %all-gather.32.cloned.1.call-start = ((), (), s32[]{:S(2)}) async-start(), calls=%async_computation.30 | async-start | bytes 10485760 | tf_op jit(solution)/shard_map/all_gather | solution.py:313
  1024.2 121.7 %all-to-all-start.7 = ((bf16[2,640,2048]{2,0,1:T(2,128)(2,1)}), bf16[2,640,2048]{2,0,1:T(2,128)(2,1)}, u32[]{:S(2)}, u32[]{:S(2)}) async-start(bf16[2,640,2048]{2,0,1:T(2,128)(2,1)} %copy.597), calls=%async_computation.7 | async-start | bytes 10485760 | tf_op jit(solution)/shard_map/all_to_all | solution.py:500
  1111.5 39.1 %copy-start.32 = (s32[128,8]{1,0:T(8,128)S(1)}, s32[128,8]{1,0:T(8,128)}, u32[]{:S(2)}) copy-start(s32[128,8]{1,0:T(8,128)} %copy-done.31) | copy-start | bytes 12292
  1145.9 121.1 %all-to-all-start.5 = ((bf16[2,640,2048]{2,0,1:T(2,128)(2,1)}), bf16[2,640,2048]{2,0,1:T(2,128)(2,1)}, u32[]{:S(2)}, u32[]{:S(2)}) async-start(bf16[2,640,2048]{2,0,1:T(2,128)(2,1)} %copy.591), calls=%async_computation.5 | async-start | bytes 10485760 | tf_op jit(solution)/shard_map/all_to_all | solution.py:437
  1150.6 215.3 %all-gather.40.cloned.1.call-start = ((), (), s32[]{:S(2)}) async-start(), calls=%async_computation.34 | async-start | bytes 4718592 | tf_op jit(solution)/shard_map/all_gather | solution.py:304
  1321.0 92.1 %all-gather.42.cloned.1.call-start = ((), (), s32[]{:S(2)}) async-start(), calls=%async_computation.35 | async-start | bytes 4718592 | tf_op jit(solution)/shard_map/all_gather | solution.py:305
  1321.5 519.6 %reduce-scatter.13.cloned.1.call-start = ((), (), s32[]{:S(2)}) async-start(), calls=%async_computation.36 | async-start | bytes 4718592 | tf_op jit(solution)/shard_map/reduce_scatter | solution.py:543
  1325.4 88.7 %copy-start.40 = (s32[2,256]{1,0:T(2,128)S(1)}, s32[2,256]{1,0:T(2,128)}, u32[]{:S(2)}) copy-start(s32[2,256]{1,0:T(2,128)} %copy-done.39) | copy-start | bytes 6148
  1325.4 88.7 %copy-start.42 = (s32[2,256]{1,0:T(2,128)S(1)}, s32[2,256]{1,0:T(2,128)}, u32[]{:S(2)}) copy-start(s32[2,256]{1,0:T(2,128)} %copy-done.41) | copy-start | bytes 6148
  1776.7 110.6 %reduce-scatter.15.cloned.1.call-start = ((), (), s32[]{:S(2)}) async-start(), calls=%async_computation.37 | async-start | bytes 4718592 | tf_op jit(solution)/shard_map/reduce_scatter | solution.py:546
  1777.3 236.8 %reduce-scatter.31.cloned.1.call-start = ((), (), s32[]{:S(2)}) async-start(), calls=%async_computation.45 | async-start | bytes 1081344
  1779.1 320.7 %reduce-scatter.29.cloned.1.call-start = ((), (), s32[]{:S(2)}) async-start(), calls=%async_computation.44 | async-start | bytes 10485760 | tf_op jit(solution)/shard_map/reduce_scatter | solution.py:496
  1793.4 395.8 %reduce-scatter.25.cloned.1.call-start = ((), (), s32[]{:S(2)}) async-start(), calls=%async_computation.42 | async-start | bytes 10485760 | tf_op jit(solution)/shard_map/reduce_scatter | solution.py:490
  1806.7 471.7 %reduce-scatter.27.cloned.1.call-start = ((), (), s32[]{:S(2)}) async-start(), calls=%async_computation.43 | async-start | bytes 10485760 | tf_op jit(solution)/shard_map/reduce_scatter | solution.py:493
  1820.0 649.0 %reduce-scatter.23.cloned.1.call-start = ((), (), s32[]{:S(2)}) async-start(), calls=%async_computation.41 | async-start | bytes 17301504 | tf_op jit(solution)/shard_map/reduce_scatter | solution.py:590
  1841.1 10.0 all-to-all-start.10
  1844.6 811.6 %reduce-scatter.19.cloned.1.call-start = ((), (), s32[]{:S(2)}) async-start(), calls=%async_computation.39 | async-start | bytes 17301504 | tf_op jit(solution)/shard_map/reduce_scatter | solution.py:588
  1870.4 973.0 %reduce-scatter.17.cloned.1.call-start = ((), (), s32[]{:S(2)}) async-start(), calls=%async_computation.38 | async-start | bytes 17301504 | tf_op jit(solution)/shard_map/reduce_scatter | solution.py:587
  1887.3 1143.2 %reduce-scatter.21.cloned.1.call-start = ((), (), s32[]{:S(2)}) async-start(), calls=%async_computation.40 | async-start | bytes 17301504 | tf_op jit(solution)/shard_map/reduce_scatter | solution.py:589
  2292.1 48.0 %copy-start.60 = (f32[128]{0:T(128)S(1)}, f32[128]{0:T(128)}, u32[]{:S(2)}) copy-start(f32[128]{0:T(128)} %copy-done.59) | copy-start | bytes 1540
  (67 other events, 487.2 us)
Sparse Core Ops, SparseCore 0:
  11.0 80.0 all-gather.15
  94.1 75.6 all-gather.17
  172.8 78.9 all-gather.21
  253.8 45.7 all-gather.19
  301.0 46.1 all-gather.23
  350.0 75.8 all-gather.25
  427.8 86.1 all-gather.27
  515.8 93.0 all-gather.29
  737.0 85.4 all-gather.33
  824.2 87.4 all-gather.35
  913.5 87.4 all-gather.37
  1002.8 87.4 all-gather.31
  1321.1 44.7 all-gather.39
  1367.3 45.6 all-gather.41
  1776.9 48.7 reduce-scatter.12
  1828.4 48.3 reduce-scatter.14
  1878.8 135.2 reduce-scatter.30
  2017.0 82.7 reduce-scatter.28
  2102.9 86.3 reduce-scatter.24
  2192.1 86.2 reduce-scatter.26
  2281.3 187.6 reduce-scatter.22
  2471.8 184.3 reduce-scatter.18
  2659.1 184.2 reduce-scatter.16
  2846.1 184.3 reduce-scatter.20
where the time goes:
time: 3050 us; the launch traced here: 3040 us
  waiting for transfers between devices  1690 us (55%)
  local copies, waits for them, and re-layouts  308 us (10%)
  blocking collectives  304 us (10%)
  loops' own time  245 us (8%)
  matrix products  235 us (8%)
  other arithmetic  212 us (7%)
    reduce_scatter x1, waiting for transfers between devices, on_device(): lax.psum_scatter(key_sum, ('head', 'blk'), scatter_dimension=0, tiled=True)  187 us
    reduce_scatter x1, waiting for transfers between devices, on_device(): lax.psum_scatter(query_sum, ('head', 'blk'), scatter_dimension=0, tiled=T...  187 us
    reduce_scatter x1, waiting for transfers between devices, on_device(): lax.psum_scatter(value_sum, ('head', 'blk'), scatter_dimension=0, tiled=T...  187 us
    reduce_scatter x1, waiting for transfers between devices, on_device(): lax.psum_scatter(output_sum, ('head', 'blk'), scatter_dimension=0, tiled=...  126 us
    another operation x1, loops' own time, attend_forward(): (sums, totals), unused = lax.scan(visit, initial, key_stack)  122 us
    another operation x1, loops' own time, attend_backward(): lax.scan(visit, jnp.zeros((2, half_rows, columns), jnp.float32), key_stack)  121 us
    all_to_all x1, blocking collectives, on_device(): lax.all_to_all(pair_buffer.reshape(local_experts, per_source, width), 'bl...  121 us
    all_to_all x1, waiting for transfers between devices, on_device(): lax.all_to_all(outgoing.reshape(local_experts, per_source, width), 'blk',...  116 us
  transfers between devices with their start and end apart: 30, of which 21 were waited for; matrix products, arithmetic and copies ran while one was open for 15% of the time, Pallas kernels for 0%

commit v1 on v0

v1 whole, which is shorter than its diff:
```python
from functools import partial
import math

import jax
import jax.numpy as jnp
from jax import lax
from jax.sharding import PartitionSpec as P

HDIM = 128


norm_eps = 1e-05
rope_base = 10000.0


def rms_factor(square_sum, width):
    return lax.rsqrt(square_sum / width + norm_eps)


def rope_tables(position, head_size):
    half = head_size // 2
    freqs = rope_base ** (-(jnp.arange(half, dtype=jnp.float32) * 2.0) / head_size)
    angles = position.astype(jnp.float32)[:, None] * freqs[None, :]
    return (jnp.cos(angles)[:, None, :], jnp.sin(angles)[:, None, :])


def rotate(value, cosine, sine_part):
    half = cosine.shape[-1]
    shaped = value.reshape(value.shape[0], -1, 2 * half)
    former = shaped[:, :, :half]
    latter = shaped[:, :, half:]
    turned = jnp.concatenate(
        [former * cosine - latter * sine_part, latter * cosine + former * sine_part], axis=-1
    )
    return turned.reshape(value.shape)


def slot_codes(routes, ordering, experts, capacity):
    expert_ids = jnp.arange(experts, dtype=jnp.int32)
    absent = jnp.int32(1 << 30)
    chosen = routes[:, :, None] == expert_ids[None, None, :]
    order = jnp.min(jnp.where(chosen, ordering[:, :, None], absent), axis=1)
    rank = jnp.sum((order[None, :, :] < order[:, None, :]).astype(jnp.int32), axis=1)
    return jnp.where((order < absent) & (rank < capacity), rank, -1)


def stream_layout(seq_lengths, stream_index):
    ends = jnp.cumsum(seq_lengths)
    starts = ends - seq_lengths
    passed = (stream_index[:, None] >= ends[None, :]).astype(jnp.int32)
    sequence = jnp.sum(passed, axis=1)
    owner = sequence[:, None] == jnp.arange(seq_lengths.shape[0], dtype=jnp.int32)[None, :]
    opening = jnp.sum(jnp.where(owner, starts[None, :], 0), axis=1)
    return (sequence, stream_index - opening)


def scores_of(queries, keys, head_size):
    heads = queries.shape[1] // head_size
    query_heads = queries.reshape(queries.shape[0], heads, head_size)
    key_heads = keys.reshape(keys.shape[0], heads, head_size)
    return jnp.einsum(
        "qhd,khd->hqk", query_heads, key_heads, preferred_element_type=jnp.float32
    ) * (1.0 / math.sqrt(head_size))


def allowed_pairs(query_index, query_seq, key_index, key_seq):
    return (query_seq[:, None] == key_seq[None, :]) & (key_index[None, :] <= query_index[:, None])


def any_allowed(query_index, query_seq, key_index, key_seq):
    early = jnp.min(key_index) <= jnp.max(query_index)
    above = jnp.max(key_seq) >= jnp.min(query_seq)
    below = jnp.min(key_seq) <= jnp.max(query_seq)
    return early & above & below


def pair_forward(head_size, operands):
    queries, keys, values, query_index, query_seq, key_index, key_seq = operands
    scores = scores_of(queries, keys, head_size)
    allowed = allowed_pairs(query_index, query_seq, key_index, key_seq)
    expo = jnp.where(allowed[None], jnp.exp(scores), 0.0)
    heads = scores.shape[0]
    value_heads = values.reshape(values.shape[0], heads, head_size)
    summed = jnp.einsum(
        "hqk,khd->qhd", expo.astype(jnp.bfloat16), value_heads, preferred_element_type=jnp.float32
    )
    return (summed.reshape(queries.shape[0], queries.shape[1]), jnp.sum(expo, axis=-1))


def pair_forward_skip(head_size, operands):
    queries = operands[0]
    heads = queries.shape[1] // head_size
    return (
        jnp.zeros(queries.shape, jnp.float32),
        jnp.zeros((heads, queries.shape[0]), jnp.float32),
    )


def pair_backward(head_size, operands):
    queries, keys, values, scaled_grad, correction, query_index, query_seq, key_index, key_seq = (
        operands
    )
    scores = scores_of(queries, keys, head_size)
    allowed = allowed_pairs(query_index, query_seq, key_index, key_seq)
    expo = jnp.where(allowed[None], jnp.exp(scores), 0.0)
    heads = scores.shape[0]
    query_count = queries.shape[0]
    key_count = keys.shape[0]
    query_heads = queries.reshape(query_count, heads, head_size)
    key_heads = keys.reshape(key_count, heads, head_size)
    value_heads = values.reshape(key_count, heads, head_size)
    grad_heads = scaled_grad.reshape(query_count, heads, head_size)
    prob_grad = jnp.einsum(
        "qhd,khd->hqk", grad_heads, value_heads, preferred_element_type=jnp.float32
    )
    score_grad = (expo * (prob_grad - correction[:, :, None])).astype(jnp.bfloat16)
    factor = 1.0 / math.sqrt(head_size)
    query_part = (
        jnp.einsum("hqk,khd->qhd", score_grad, key_heads, preferred_element_type=jnp.float32)
        * factor
    )
    key_part = (
        jnp.einsum("hqk,qhd->khd", score_grad, query_heads, preferred_element_type=jnp.float32)
        * factor
    )
    value_part = jnp.einsum(
        "hqk,qhd->khd", expo.astype(jnp.bfloat16), grad_heads, preferred_element_type=jnp.float32
    )
    return (
        query_part.reshape(queries.shape),
        key_part.reshape(keys.shape),
        value_part.reshape(keys.shape),
    )


def pair_backward_skip(head_size, operands):
    queries = operands[0]
    keys = operands[1]
    return (
        jnp.zeros(queries.shape, jnp.float32),
        jnp.zeros(keys.shape, jnp.float32),
        jnp.zeros(keys.shape, jnp.float32),
    )


def attend_forward(queries, keys, values, query_index, query_seq, key_index, key_seq, head_size):
    rows, columns = queries.shape
    heads = columns // head_size
    half_rows = rows // 2
    groups = keys.shape[0] // rows
    query_blocks = queries.reshape(2, half_rows, columns)
    query_marks = query_index.reshape(2, half_rows)
    query_seqs = query_seq.reshape(2, half_rows)
    key_stack = (
        keys.reshape(groups, 2, half_rows, columns),
        values.reshape(groups, 2, half_rows, columns),
        key_index.reshape(groups, 2, half_rows),
        key_seq.reshape(groups, 2, half_rows),
    )

    def visit(carry, group):
        sums, totals = carry
        group_keys, group_values, group_index, group_seq = group
        sum_list = []
        total_list = []
        for query_part in range(2):
            running = sums[query_part]
            counted = totals[query_part]
            for key_part in range(2):
                operands = (
                    query_blocks[query_part],
                    group_keys[key_part],
                    group_values[key_part],
                    query_marks[query_part],
                    query_seqs[query_part],
                    group_index[key_part],
                    group_seq[key_part],
                )
                living = any_allowed(
                    query_marks[query_part],
                    query_seqs[query_part],
                    group_index[key_part],
                    group_seq[key_part],
                )
                add_sum, add_total = lax.cond(
                    living,
                    partial(pair_forward, head_size),
                    partial(pair_forward_skip, head_size),
                    operands,
                )
                running = running + add_sum
                counted = counted + add_total
            sum_list.append(running)
            total_list.append(counted)
        return ((jnp.stack(sum_list), jnp.stack(total_list)), None)

    initial = (
        jnp.zeros((2, half_rows, columns), jnp.float32),
        jnp.zeros((2, heads, half_rows), jnp.float32),
    )
    (sums, totals), unused = lax.scan(visit, initial, key_stack)
    totals_rows = jnp.transpose(totals, (1, 0, 2)).reshape(heads, rows)
    attended = sums.reshape(rows, heads, head_size) / jnp.transpose(totals_rows)[:, :, None]
    return (attended.reshape(rows, columns), totals_rows)


def attend_backward(
    queries,
    keys,
    values,
    scaled_grad,
    correction,
    query_index,
    query_seq,
    key_index,
    key_seq,
    head_size,
):
    rows, columns = queries.shape
    heads = columns // head_size
    half_rows = rows // 2
    groups = keys.shape[0] // rows
    query_blocks = queries.reshape(2, half_rows, columns)
    scaled_blocks = scaled_grad.reshape(2, half_rows, columns)
    correction_blocks = jnp.transpose(correction.reshape(heads, 2, half_rows), (1, 0, 2))
    query_marks = query_index.reshape(2, half_rows)
    query_seqs = query_seq.reshape(2, half_rows)
    key_stack = (
        keys.reshape(groups, 2, half_rows, columns),
        values.reshape(groups, 2, half_rows, columns),
        key_index.reshape(groups, 2, half_rows),
        key_seq.reshape(groups, 2, half_rows),
    )

    def visit(carry, group):
        group_keys, group_values, group_index, group_seq = group
        key_list = [
            jnp.zeros((half_rows, columns), jnp.float32),
            jnp.zeros((half_rows, columns), jnp.float32),
        ]
        value_list = [
            jnp.zeros((half_rows, columns), jnp.float32),
            jnp.zeros((half_rows, columns), jnp.float32),
        ]
        query_list = []
        for query_part in range(2):
            running = carry[query_part]
            for key_part in range(2):
                operands = (
                    query_blocks[query_part],
                    group_keys[key_part],
                    group_values[key_part],
                    scaled_blocks[query_part],
                    correction_blocks[query_part],
                    query_marks[query_part],
                    query_seqs[query_part],
                    group_index[key_part],
                    group_seq[key_part],
                )
                living = any_allowed(
                    query_marks[query_part],
                    query_seqs[query_part],
                    group_index[key_part],
                    group_seq[key_part],
                )
                add_query, add_key, add_value = lax.cond(
                    living,
                    partial(pair_backward, head_size),
                    partial(pair_backward_skip, head_size),
                    operands,
                )
                running = running + add_query
                key_list[key_part] = key_list[key_part] + add_key
                value_list[key_part] = value_list[key_part] + add_value
            query_list.append(running)
        return (jnp.stack(query_list), (jnp.stack(key_list), jnp.stack(value_list)))

    query_grad, (key_grads, value_grads) = lax.scan(
        visit, jnp.zeros((2, half_rows, columns), jnp.float32), key_stack
    )
    return (
        query_grad.reshape(rows, columns),
        key_grads.reshape(groups * rows, columns),
        value_grads.reshape(groups * rows, columns),
    )


def on_device(
    tokens,
    query_weight,
    key_weight,
    value_weight,
    output_weight,
    mixing_gain,
    query_gain,
    key_gain,
    routing_gain,
    router_weight,
    gate_weight,
    up_weight,
    down_weight,
    seq_lengths,
    dealt_order,
    expert_routes,
    slot_order,
    cotangent,
):
    heads_axis = lax.axis_size("head")
    blocks = lax.axis_size("blk")
    head_at = lax.axis_index("head")
    block_at = lax.axis_index("blk")
    rows, width = tokens.shape
    picks = expert_routes.shape[1]
    total_rows = dealt_order.shape[0]
    group = rows * heads_axis
    columns = width // heads_axis
    part = query_weight.shape[0]
    head_size = HDIM
    heads_here = columns // head_size
    f32 = jnp.float32
    bf16 = jnp.bfloat16
    experts = router_weight.shape[1]
    local_experts = gate_weight.shape[0]
    capacity = 5 * rows * picks // (4 * experts)

    small = jnp.concatenate(
        [
            mixing_gain[:, None],
            query_gain[:, None],
            key_gain[:, None],
            routing_gain[:, None],
            router_weight,
        ],
        axis=1,
    ).reshape(1, -1)
    small_all = lax.all_gather(small, ("head", "blk"), axis=0, tiled=True).reshape(
        width, 4 + experts
    )
    mixing_scale = small_all[:, 0].astype(f32)
    routing_scale = small_all[:, 3].astype(f32)
    query_scale = lax.dynamic_slice_in_dim(small_all[:, 1], head_at * columns, columns).astype(f32)
    key_scale = lax.dynamic_slice_in_dim(small_all[:, 2], head_at * columns, columns).astype(f32)
    router_full = small_all[:, 4:]
    codes = slot_codes(expert_routes, slot_order, experts, capacity)
    codes_all = lax.all_gather(codes, "blk", axis=0, tiled=True).reshape(blocks, rows, experts)
    codes_here = lax.dynamic_slice_in_dim(codes_all, block_at * local_experts, local_experts, 2)

    key_index = jnp.transpose(
        dealt_order.reshape(heads_axis, blocks, rows), (1, 0, 2)
    ).reshape(total_rows)
    key_seq = stream_layout(seq_lengths, key_index)[0]
    query_index = lax.dynamic_slice_in_dim(key_index, block_at * group, group)
    query_seq, query_position = stream_layout(seq_lengths, query_index)
    cosine, sine_part = rope_tables(query_position, head_size)

    tokens_group = lax.all_gather(tokens, "head", axis=0, tiled=True).astype(f32)
    stacked = jnp.stack([query_weight, key_weight, value_weight])
    turned = lax.all_to_all(stacked, "head", split_axis=2, concat_axis=1, tiled=True)
    gathered = lax.all_gather(turned, "blk", axis=1, tiled=False)
    gathered = jnp.transpose(
        gathered.reshape(3, blocks, heads_axis, part, columns), (0, 2, 1, 3, 4)
    ).reshape(3, width, columns)
    output_rows = lax.all_gather(output_weight, "blk", axis=0, tiled=True)
    cot_all = lax.all_gather(cotangent, "blk", axis=0, tiled=True).reshape(blocks, rows, width)
    token_factor = rms_factor(jnp.sum(tokens_group * tokens_group, axis=-1, keepdims=True), width)
    normed = (tokens_group * token_factor * mixing_scale).astype(bf16)
    query_raw = jnp.dot(normed, gathered[0], preferred_element_type=f32)
    key_raw = jnp.dot(normed, gathered[1], preferred_element_type=f32)
    value_heads = jnp.dot(normed, gathered[2], preferred_element_type=f32).astype(bf16)
    squares = lax.psum(
        jnp.stack([jnp.sum(query_raw * query_raw, axis=-1), jnp.sum(key_raw * key_raw, axis=-1)]),
        "head",
    )
    query_factor = rms_factor(squares[0][:, None], width)
    key_factor = rms_factor(squares[1][:, None], width)
    query_heads = rotate(query_raw * query_factor * query_scale, cosine, sine_part).astype(bf16)
    key_heads = rotate(key_raw * key_factor * key_scale, cosine, sine_part).astype(bf16)
    keys_all = lax.all_gather(key_heads, "blk", axis=0, tiled=True)
    values_all = lax.all_gather(value_heads, "blk", axis=0, tiled=True)
    attended, totals = attend_forward(
        query_heads, keys_all, values_all, query_index, query_seq, key_index, key_seq, head_size
    )
    context = attended.astype(bf16)
    branch = jnp.dot(context, output_rows, preferred_element_type=f32).astype(bf16)
    branch_parts = lax.all_to_all(
        branch.reshape(heads_axis, rows, width), "head", split_axis=0, concat_axis=0, tiled=True
    )
    own_tokens = tokens.astype(f32)
    middle = own_tokens + jnp.sum(branch_parts.astype(f32), axis=0)
    middle_factor = rms_factor(jnp.sum(middle * middle, axis=-1, keepdims=True), width)
    routed = (middle * middle_factor * routing_scale).astype(bf16)
    probs = jax.nn.softmax(jnp.dot(routed, router_full, preferred_element_type=f32), axis=-1)

    routed_all = lax.all_gather(routed, "blk", axis=0, tiled=True)
    probs_all = jax.nn.softmax(
        jnp.dot(routed_all, router_full, preferred_element_type=f32), axis=-1
    )
    weight_here = lax.dynamic_slice_in_dim(
        probs_all, block_at * local_experts, local_experts, 1
    ).reshape(blocks, rows, local_experts)
    routed_all = routed_all.reshape(blocks, rows, width)
    slot_ids = jnp.arange(capacity, dtype=jnp.int32)
    placed = (
        jnp.transpose(codes_here, (2, 0, 1))[:, :, None, :] == slot_ids[None, None, :, None]
    )
    place = placed.astype(bf16)
    slot_weight = jnp.sum(
        jnp.where(placed, jnp.transpose(weight_here, (2, 0, 1))[:, :, None, :], 0.0), axis=-1
    )
    slots = blocks * capacity
    arrived = jnp.einsum("lsrt,std->lsrd", place, routed_all).reshape(local_experts, slots, width)
    arrived_cot = jnp.einsum("lsrt,std->lsrd", place, cot_all).reshape(local_experts, slots, width)
    slot_weight = slot_weight.reshape(local_experts, slots, 1)
    gate_all = lax.all_gather(gate_weight, "head", axis=1, tiled=True)
    up_all = lax.all_gather(up_weight, "head", axis=1, tiled=True)
    down_all = lax.all_gather(down_weight, "head", axis=1, tiled=True)
    gate = jnp.einsum("esd,edf->esf", arrived, gate_all, preferred_element_type=f32)
    upward = jnp.einsum("esd,edf->esf", arrived, up_all, preferred_element_type=f32)
    sigmoid = jax.nn.sigmoid(gate)
    active = (gate * sigmoid * upward).astype(bf16)
    produced = jnp.einsum("esf,efd->esd", active, down_all, preferred_element_type=f32).astype(bf16)
    cot_float = arrived_cot.astype(f32)
    produced_float = produced.astype(f32)
    weighted = (slot_weight * produced_float).astype(bf16).reshape(
        local_experts, blocks, capacity, width
    )
    combined = jnp.einsum("lsrt,lsrd->std", place, weighted, preferred_element_type=f32)
    combined = lax.psum_scatter(
        combined.astype(bf16).reshape(blocks * rows, width), "blk", scatter_dimension=0, tiled=True
    )
    block_output = (middle + combined.astype(f32)).astype(bf16)
    slot_grad = jnp.sum(cot_float * produced_float, axis=-1).reshape(
        local_experts, blocks, capacity, 1
    )
    weight_grad = jnp.transpose(
        jnp.sum(jnp.where(placed, slot_grad, 0.0), axis=2), (1, 2, 0)
    )
    prob_grad = lax.all_to_all(weight_grad, "blk", split_axis=0, concat_axis=2, tiled=True).reshape(
        rows, experts
    )
    produced_grad = (slot_weight * cot_float).astype(bf16)
    active_grad = jnp.einsum("esd,efd->esf", produced_grad, down_all, preferred_element_type=f32)
    gate_grad = (active_grad * upward * sigmoid * (1.0 + gate * (1.0 - sigmoid))).astype(bf16)
    up_grad = (active_grad * (gate * sigmoid)).astype(bf16)
    incoming = jnp.einsum("esf,edf->esd", gate_grad, gate_all, preferred_element_type=f32)
    incoming = incoming + jnp.einsum("esf,edf->esd", up_grad, up_all, preferred_element_type=f32)
    incoming = incoming.astype(bf16).reshape(local_experts, blocks, capacity, width)
    incoming = jnp.einsum("lsrt,lsrd->std", place, incoming, preferred_element_type=f32)
    routed_grad = lax.psum_scatter(
        incoming.astype(bf16).reshape(blocks * rows, width), "blk", scatter_dimension=0, tiled=True
    ).astype(f32)
    down_sum = jnp.einsum("esf,esd->efd", active, produced_grad, preferred_element_type=f32)
    gate_sum = jnp.einsum("esd,esf->edf", arrived, gate_grad, preferred_element_type=f32)
    up_sum = jnp.einsum("esd,esf->edf", arrived, up_grad, preferred_element_type=f32)
    gate_out, up_out, down_out = (
        lax.psum_scatter(item.astype(bf16), "head", scatter_dimension=1, tiled=True).astype(f32)
        for item in (gate_sum, up_sum, down_sum)
    )

    logit_grad = (
        probs * (prob_grad - jnp.sum(probs * prob_grad, axis=1, keepdims=True))
    ).astype(bf16)
    router_sum = jnp.dot(routed.T, logit_grad, preferred_element_type=f32)
    routed_grad = routed_grad + jnp.dot(logit_grad, router_full.T, preferred_element_type=f32)
    scaled = routed_grad * routing_scale
    inner = jnp.mean(scaled * middle, axis=-1, keepdims=True)
    middle_grad = (
        cotangent.astype(f32) + middle_factor * scaled - middle * (middle_factor**3 * inner)
    )
    routing_sum = jnp.sum(routed_grad * middle * middle_factor, axis=0)

    branch_grad = lax.all_gather(middle_grad.astype(bf16), "head", axis=0, tiled=True)
    context_grad = jnp.dot(branch_grad, output_rows.T, preferred_element_type=f32).astype(bf16)
    output_sum = jnp.dot(context.T, branch_grad, preferred_element_type=f32).astype(bf16)
    output_out = lax.psum_scatter(output_sum, "blk", scatter_dimension=0, tiled=True).astype(f32)
    context_float = context_grad.astype(f32).reshape(group, heads_here, head_size)
    scaled_grad = (
        (context_float / jnp.transpose(totals)[:, :, None]).astype(bf16).reshape(group, columns)
    )
    correction = (
        jnp.transpose(
            jnp.sum(context_float * attended.reshape(group, heads_here, head_size), axis=2)
        )
        / totals
    )
    query_grad_heads, key_grad_all, value_grad_all = attend_backward(
        query_heads,
        keys_all,
        values_all,
        scaled_grad,
        correction,
        query_index,
        query_seq,
        key_index,
        key_seq,
        head_size,
    )
    key_back = lax.psum_scatter(key_grad_all.astype(bf16), "blk", scatter_dimension=0, tiled=True)
    value_back = lax.psum_scatter(
        value_grad_all.astype(bf16), "blk", scatter_dimension=0, tiled=True
    )
    query_turn = rotate(query_grad_heads.astype(bf16).astype(f32), cosine, -sine_part)
    key_turn = rotate(key_back.astype(f32), cosine, -sine_part)
    query_scaled = query_turn * query_scale
    key_scaled = key_turn * key_scale
    inners = (
        lax.psum(
            jnp.stack(
                [jnp.sum(query_scaled * query_raw, axis=-1), jnp.sum(key_scaled * key_raw, axis=-1)]
            ),
            "head",
        )
        / width
    )
    query_raw_grad = (
        query_factor * query_scaled - query_raw * (query_factor**3 * inners[0][:, None])
    ).astype(bf16)
    key_raw_grad = (
        key_factor * key_scaled - key_raw * (key_factor**3 * inners[1][:, None])
    ).astype(bf16)
    querynorm_sum = jnp.sum(query_turn * query_raw * query_factor, axis=0)
    keynorm_sum = jnp.sum(key_turn * key_raw * key_factor, axis=0)
    normed_part = jnp.dot(query_raw_grad, gathered[0].T, preferred_element_type=f32)
    normed_part = normed_part + jnp.dot(key_raw_grad, gathered[1].T, preferred_element_type=f32)
    normed_part = normed_part + jnp.dot(value_back, gathered[2].T, preferred_element_type=f32)
    normed_parts = lax.all_to_all(
        normed_part.astype(bf16).reshape(heads_axis, rows, width),
        "head",
        split_axis=0,
        concat_axis=0,
        tiled=True,
    )
    normed_grad = jnp.sum(normed_parts.astype(f32), axis=0)
    own_factor = rms_factor(jnp.sum(own_tokens * own_tokens, axis=-1, keepdims=True), width)
    scaled = normed_grad * mixing_scale
    inner = jnp.mean(scaled * own_tokens, axis=-1, keepdims=True)
    tokens_grad = middle_grad + own_factor * scaled - own_tokens * (own_factor**3 * inner)
    mixing_sum = jnp.sum(normed_grad * own_tokens * own_factor, axis=0)
    raw_grads = jnp.stack([query_raw_grad, key_raw_grad, value_back])
    weight_sums = jnp.einsum("td,ntc->ndc", normed, raw_grads, preferred_element_type=f32).astype(
        bf16
    )
    weight_sums = jnp.transpose(
        weight_sums.reshape(3, heads_axis, blocks, part, columns), (2, 0, 1, 3, 4)
    ).reshape(blocks * 3 * heads_axis * part, columns)
    weight_sums = lax.psum_scatter(weight_sums, "blk", scatter_dimension=0, tiled=True)
    weight_sums = lax.all_to_all(
        weight_sums.reshape(3, heads_axis * part, columns),
        "head",
        split_axis=1,
        concat_axis=2,
        tiled=True,
    ).astype(f32)
    blank = jnp.zeros((heads_axis, columns), f32)
    query_line = lax.dynamic_update_slice(blank, querynorm_sum[None], (head_at, 0)).reshape(width)
    key_line = lax.dynamic_update_slice(blank, keynorm_sum[None], (head_at, 0)).reshape(width)
    lines = jnp.concatenate(
        [
            mixing_sum[:, None],
            query_line[:, None],
            key_line[:, None],
            routing_sum[:, None],
            router_sum,
        ],
        axis=1,
    )
    lines = jnp.pad(
        lines.reshape(heads_axis * blocks, -1), ((0, 0), (0, -part * (4 + experts) % 1024))
    ).reshape(-1, 128)
    lines = lax.psum_scatter(lines, ("head", "blk"), scatter_dimension=0, tiled=True).reshape(
        -1
    )[: part * (4 + experts)].reshape(part, 4 + experts)
    return (
        block_output,
        tokens_grad,
        weight_sums[0],
        weight_sums[1],
        weight_sums[2],
        output_out,
        lines[:, 0],
        lines[:, 1],
        lines[:, 2],
        lines[:, 3],
        lines[:, 4:],
        gate_out,
        up_out,
        down_out,
    )


def solution(mesh):
    in_specs = (
        P(("head", "blk"), None),
        P(("head", "blk"), None),
        P(("head", "blk"), None),
        P(("head", "blk"), None),
        P(("head", "blk"), None),
        P(("head", "blk")),
        P(("head", "blk")),
        P(("head", "blk")),
        P(("head", "blk")),
        P(("head", "blk"), None),
        P("blk", "head", None),
        P("blk", "head", None),
        P("blk", "head", None),
        P(),
        P(),
        P(("head", "blk"), None),
        P(("head", "blk"), None),
        P(("head", "blk"), None),
    )
    out_specs = (
        P(("head", "blk"), None),
        P(("head", "blk"), None),
        P(("head", "blk"), None),
        P(("head", "blk"), None),
        P(("head", "blk"), None),
        P(("head", "blk"), None),
        P(("head", "blk")),
        P(("head", "blk")),
        P(("head", "blk")),
        P(("head", "blk")),
        P(("head", "blk"), None),
        P("blk", "head", None),
        P("blk", "head", None),
        P("blk", "head", None),
    )
    return jax.shard_map(
        on_device, mesh=mesh, in_specs=in_specs, out_specs=out_specs, check_vma=False
    )
```

time: 3050 us -> 2010 us (0.66)
  waiting for transfers between devices: 1690 us -> 960 us
  blocking collectives: 304 us -> 128 us
  local copies, waits for them, and re-layouts: 308 us -> 250 us
  other arithmetic: 212 us -> 170 us
    reduce_scatter x9 -> x10, waiting for transfers between devices: 943 us -> 556 us  [the longest x3 269 us: on_device(): lax.psum_scatter(item.astype(bf16), 'head', scatter_dimension=1, tiled=True)]
    all_to_all x6 -> x3, waiting for transfers between devices: 266 us -> 5.73 us  [the longest x1 5.73 us: on_device(): lax.all_to_all(weight_grad, 'blk', split_axis=0, concat_axis=2, tiled=True)]
    all_to_all x6 -> x2, blocking collectives: 177 us -> 52 us  [the longest x1 29.8 us: on_device(): lax.all_to_all(branch.reshape(heads_axis, rows, width), 'head', split_axi...]
    unnamed x25 -> x21, waiting for transfers between devices: 114 us -> 3.9 us
    unnamed x2 -> x0, blocking collectives: 84.5 us -> none
    all_gather x14 -> x11, waiting for transfers between devices: 369 us -> 394 us  [the longest x1 81.4 us: on_device(): gate_all = lax.all_gather(gate_weight, 'head', axis=1, tiled=True)]
    dot_general x23 -> x27, matrix products: 189 us -> 165 us  [the longest x1 15.5 us: on_device(): jnp.einsum('esd,efd->esf', produced_grad, down_all, preferred_element_typ...]
    another operation x121 -> x118, local copies, waits for them, and re-layouts: 61.9 us -> 63.4 us
  transfers between devices with their start and end apart: 30 -> 24, of which waited for: 21 -> 17; matrix products, arithmetic and copies ran while one was open for 15% -> 14% of each run, Pallas kernels for 0% -> 0%
where the time goes in v1:
time: 2010 us; the launch traced here: 2000 us
  waiting for transfers between devices  960 us (48%)
  local copies, waits for them, and re-layouts  250 us (12%)
  loops' own time  247 us (12%)
  matrix products  211 us (10%)
  other arithmetic  170 us (8%)
  blocking collectives  128 us (6%)
    reduce_scatter x3, waiting for transfers between devices, on_device(): lax.psum_scatter(item.astype(bf16), 'head', scatter_dimension=1, tiled=True)  269 us
    reduce_scatter x1, waiting for transfers between devices, on_device(): lax.psum_scatter(lines, ('head', 'blk'), scatter_dimension=0, tiled=True)  133 us
    another operation x1, loops' own time, attend_forward(): (sums, totals), unused = lax.scan(visit, initial, key_stack)  124 us
    another operation x1, loops' own time, attend_backward(): lax.scan(visit, jnp.zeros((2, half_rows, columns), jnp.float32), key_stack)  122 us
    all_gather x1, waiting for transfers between devices, on_device(): gate_all = lax.all_gather(gate_weight, 'head', axis=1, tiled=True)  81.4 us
    all_gather x1, waiting for transfers between devices, on_device(): up_all = lax.all_gather(up_weight, 'head', axis=1, tiled=True)  77.8 us
    all_gather x1, waiting for transfers between devices, on_device(): down_all = lax.all_gather(down_weight, 'head', axis=1, tiled=True)  76.1 us
    another operation x117, local copies, waits for them, and re-layouts  62 us
  transfers between devices with their start and end apart: 24, of which 17 were waited for; matrix products, arithmetic and copies ran while one was open for 14% of the time, Pallas kernels for 0%

profile of v1, /device:TPU:0, one launch (start us, length us, event | category | flops | bytes accessed | tf_op | source)
XLA Modules:
  0.0 1996.8 jit_solution(6454628020180375164)
XLA Ops:
  12.1 22.2 %all_to_all.49 = bf16[4,2,49152]{2,1,0:T(2,128)(2,1)} all-to-all(bf16[4,2,49152]{2,1,0:T(2,128)(2,1)S(1)} %reshape.1107), channel_id=1, replica_groups=mesh['head'=4,'blk'=8] {'head'}, dimensions={0} | all-to-all | bytes 1572864 | tf_op jit(solution)/shard_map/all_to_all | solution.py:358
  39.9 41.8 %all-gather = bf16[32,1,1280]{2,1,0:T(2,128)(2,1)S(1)} all-gather(bf16[1,1,1280]{2,1,0:T(2,128)(2,1)S(1)} %reshape.1089), channel_id=1, replica_groups=mesh['head'=4,'blk'=8] {'head','blk'}, dimensions={0}, use_global_device_ids=true | all-gather | bytes 84480 | tf_op jit(solution)/shard_map/all_gather | solution.py:336
  89.1 31.4 %all-gather.15.cloned.1.call-done = bf16[3,8,256,512]{3,2,0,1:T(8,128)(2,1)} async-done(((bf16[3,1,256,512]{3,2,0,1:T(8,128)(2,1)}), bf16[3,8,256,512]{3,2,0,1:T(8,128)(2,1)}) %all-gather.15.cloned.1.call-update) | async-done | bytes 6291472 | tf_op jit(solution)/shard_map/all_gather | solution.py:359
  131.7 10.1 psum.14
  163.3 35.6 %all-gather.17.cloned.1.call-done = bf16[4096,512]{1,0:T(8,128)(2,1)} async-done(((bf16[512,512]{1,0:T(8,128)(2,1)}), bf16[4096,512]{1,0:T(8,128)(2,1)}) %all-gather.17.cloned.1.call-update) | async-done | bytes 4194320 | tf_op jit(solution)/shard_map/all_gather | solution.py:378
  198.9 47.7 %all-gather.19.cloned.1.call-done = bf16[4096,512]{1,0:T(8,128)(2,1)} async-done(((bf16[512,512]{1,0:T(8,128)(2,1)}), bf16[4096,512]{1,0:T(8,128)(2,1)}) %all-gather.19.cloned.1.call-update) | async-done | bytes 4194320 | tf_op jit(solution)/shard_map/all_gather | solution.py:379
  247.7 194.2 %while.28 = (s32[]{:T(128)}, f32[2,256,512]{1,2,0:T(8,128)}, f32[2,4,256]{2,1,0:T(4,128)S(1)}, s32[8,2,256]{2,1,0:T(2,128)S(1)}, s32[]{:T(128)}, /*index=5*/s32[...) while((s32[]{:T(128)}, f32[2,256,512]{1,2,0:T(8,128)}, ...), condition=%wide.region_33.34_spmd, body=%wide.region_14.33_spmd.sunk | while | flops 542641664 | bytes 24740512 | solution.py:201
  447.7 29.8 %all_to_all.50 = bf16[4,128,2048]{2,1,0:T(8,128)(2,1)S(1)} all-to-all(bf16[4,128,2048]{2,1,0:T(8,128)(2,1)S(1)} %bitcast.550), channel_id=1, replica_groups=mesh['head'=4,'blk'=8] {'head'}, dimensions={0} | all-to-all | bytes 4194304 | tf_op jit(solution)/shard_map/all_to_all | solution.py:385
  484.8 14.6 all_gather.49
  508.0 16.0 all-gather.23.cloned.1.call-done
  530.8 81.4 %all-gather.25.cloned.1.call-done = bf16[2,2048,1024]{2,1,0:T(8,128)(2,1)} async-done(((bf16[2,512,1024]{2,1,0:T(8,128)(2,1)}), bf16[2,2048,1024]{2,1,0:T(8,128)(2,1)}) %all-gather.25.cloned.1.call-update) | async-done | bytes 8388624 | tf_op jit(solution)/shard_map/all_gather | solution.py:414
  612.2 11.6 fusion.168
  623.8 77.8 %all-gather.27.cloned.1.call-done = bf16[2,2048,1024]{2,1,0:T(8,128)(2,1)} async-done(((bf16[2,512,1024]{2,1,0:T(8,128)(2,1)}), bf16[2,2048,1024]{2,1,0:T(8,128)(2,1)}) %all-gather.27.cloned.1.call-update) | async-done | bytes 8388624 | tf_op jit(solution)/shard_map/all_gather | solution.py:415
  701.5 13.1 multiply_convert_fusion.2
  714.6 76.1 %all-gather.29.cloned.1.call-done = bf16[2,1024,2048]{2,1,0:T(8,128)(2,1)} async-done(((bf16[2,256,2048]{2,1,0:T(8,128)(2,1)}), bf16[2,1024,2048]{2,1,0:T(8,128)(2,1)}) %all-gather.29.cloned.1.call-update) | async-done | bytes 8388624 | tf_op jit(solution)/shard_map/all_gather | solution.py:416
  790.7 11.9 fusion.86
  807.3 9.4 fusion.87
  816.7 15.5 multiply_convert_fusion
  832.2 12.2 fusion.169
  844.5 12.4 add_convert_fusion
  856.8 5.8 bitcast_convert_fusion
  874.7 38.1 %reduce-scatter.13.cloned.1.call-done = bf16[128,2048]{1,0:T(8,128)(2,1)} async-done(((bf16[1024,2048]{1,0:T(8,128)(2,1)}), bf16[128,2048]{1,0:T(8,128)(2,1)}) %reduce-scatter.13.cloned.1.call-update) | async-done | bytes 524304 | tf_op jit(solution)/shard_map/reduce_scatter | solution.py:449
  924.1 27.8 %all-gather.33.cloned.1.call-done = bf16[512,2048]{1,0:T(8,128)(2,1)} async-done(((bf16[128,2048]{1,0:T(8,128)(2,1)}), bf16[512,2048]{1,0:T(8,128)(2,1)}) %all-gather.33.cloned.1.call-update) | async-done | bytes 2097168 | tf_op jit(solution)/shard_map/all_gather | solution.py:472
  961.2 340.6 %while.29 = (s32[]{:T(128)}, f32[2,256,512]{1,2,0:T(8,128)}, bf16[8,2,256,512]{3,2,1,0:T(8,128)(2,1)}, bf16[8,2,256,512]{2,3,1,0:T(8,128)(2,1)}, s32[8,2,256]{2,...) while((s32[]{:T(128)}, f32[2,256,512]{1,2,0:T(8,128)}, ...), condition=%wide.region_66.67_spmd, body=%wide.region_51.66_spmd.sunk | while | flops 1353451008 | bytes 68749216 | solution.py:278
  976.2 5.8 conditional.23
  988.2 5.8 conditional.22
  1023.7 5.8 conditional.23
  1184.1 5.8 conditional.23
  1196.1 5.8 conditional.22
  1230.0 5.8 conditional.23
  1242.0 5.8 conditional.22
  1302.0 8.5 copy.508
  1310.6 7.8 convert_element_type.352
  1322.8 11.9 convolution_convert_fusion
  1336.5 11.5 convolution_convert_fusion.2
  1349.8 11.6 convolution_convert_fusion.1
  1376.6 9.4 psum.15
  1388.5 12.9 reduce-scatter.17.cloned.1.call-done
  1401.4 8.2 convert_bitcast_fusion.1
  1409.6 8.7 copy.509
  1418.3 6.3 copy.510
  1425.3 5.8 bitcast_convert_fusion.1
  1445.6 98.5 %reduce-scatter.29.cloned.1.call-done = bf16[2,256,2048]{2,1,0:T(8,128)(2,1)} async-done(((bf16[2,1024,2048]{2,1,0:T(8,128)(2,1)}), bf16[2,256,2048]{2,1,0:T(8,128)(2,1)}) %reduce-scatter.29.cloned.1.call-update) | async-done | bytes 2097168 | tf_op jit(solution)/shard_map/reduce_scatter | solution.py:456
  1548.2 85.1 %reduce-scatter.25.cloned.1.call-done = bf16[2,512,1024]{2,1,0:T(8,128)(2,1)} async-done(((bf16[2,2048,1024]{2,1,0:T(8,128)(2,1)}), bf16[2,512,1024]{2,1,0:T(8,128)(2,1)}) %reduce-scatter.25.cloned.1.call-update) | async-done | bytes 2097168 | tf_op jit(solution)/shard_map/reduce_scatter | solution.py:456
  1637.4 85.2 %reduce-scatter.27.cloned.1.call-done = bf16[2,512,1024]{2,1,0:T(8,128)(2,1)} async-done(((bf16[2,2048,1024]{2,1,0:T(8,128)(2,1)}), bf16[2,512,1024]{2,1,0:T(8,128)(2,1)}) %reduce-scatter.27.cloned.1.call-update) | async-done | bytes 2097168 | tf_op jit(solution)/shard_map/reduce_scatter | solution.py:456
  1735.3 59.4 %reduce-scatter.19.cloned.1.call-done = bf16[768,512]{1,0:T(8,128)(2,1)} async-done(((bf16[6144,512]{1,0:T(8,128)(2,1)}), bf16[768,512]{1,0:T(8,128)(2,1)}) %reduce-scatter.19.cloned.1.call-update) | async-done | bytes 786448 | tf_op jit(solution)/shard_map/reduce_scatter | solution.py:546
  1801.7 43.5 %reduce-scatter.11.cloned.1.call-done = bf16[128,2048]{1,0:T(8,128)(2,1)} async-done(((bf16[1024,2048]{1,0:T(8,128)(2,1)}), bf16[128,2048]{1,0:T(8,128)(2,1)}) %reduce-scatter.11.cloned.1.call-update) | async-done | bytes 524304 | tf_op jit(solution)/shard_map/reduce_scatter | solution.py:428
  1848.4 133.4 %reduce-scatter.23.cloned.1.call-done = f32[16,128]{1,0:T(8,128)} async-done(((f32[512,128]{1,0:T(8,128)}), f32[16,128]{1,0:T(8,128)}) %reduce-scatter.23.cloned.1.call-update) | async-done | bytes 8208 | tf_op jit(solution)/shard_map/reduce_scatter | solution.py:570
  (960 shorter events, 559.2 us)
Async XLA Ops:
  7.2 79.7 %all-gather.13.cloned.1.call-start = ((), (), s32[]{:S(2)}) async-start(), calls=%async_computation.15 | async-start | bytes 2621440 | tf_op jit(solution)/shard_map/all_gather | solution.py:356
  7.9 112.6 %all-gather.15.cloned.1.call-start = ((), (), s32[]{:S(2)}) async-start(), calls=%async_computation.16 | async-start | bytes 7077888 | tf_op jit(solution)/shard_map/all_gather | solution.py:359
  12.0 27.4 %copy-start.64 = (bf16[64,16]{0,1:T(8,128)(2,1)S(1)}, bf16[64,16]{0,1:T(8,128)(2,1)}, u32[]{:S(2)}) copy-start(bf16[64,16]{0,1:T(8,128)(2,1)} %param.47) | copy-start | bytes 6148
  12.1 27.4 %copy-start.72 = (bf16[64]{0:T(256)(128)(2,1)S(1)}, bf16[64]{0:T(256)(128)(2,1)}, u32[]{:S(2)}) copy-start(bf16[64]{0:T(256)(128)(2,1)} %param.43) | copy-start | bytes 388
  34.3 49.2 %copy-start.61 = (s32[4096]{0:T(1024)S(1)}, s32[4096]{0:T(1024)}, u32[]{:S(2)}) copy-start(s32[4096]{0:T(1024)} %param.52) | copy-start | bytes 49156
  34.3 49.2 %copy-start.77 = (s32[3]{0:T(128)S(1)}, s32[3]{0:T(128)}, u32[]{:S(2)}) copy-start(s32[3]{0:T(128)} %param.51) | copy-start | bytes 40
  39.4 159.5 %all-gather.17.cloned.1.call-start = ((), (), s32[]{:S(2)}) async-start(), calls=%async_computation.17 | async-start | bytes 4718592 | tf_op jit(solution)/shard_map/all_gather | solution.py:378
  83.4 40.5 %copy-start.2 = (bf16[2048,20]{1,0:T(8,128)(2,1)}, bf16[2048,20]{1,0:T(8,128)(2,1)S(1)}, u32[]{:S(2)}) copy-start(bf16[2048,20]{1,0:T(8,128)(2,1)S(1)} %reshape.1044) | copy-start | bytes 245764
  84.2 57.7 %copy-start.57 = (f32[512]{0:T(512)}, f32[512]{0:T(512)S(1)}, u32[]{:S(2)}) copy-start(f32[512]{0:T(512)S(1)} %get-tuple-element.1029) | copy-start | bytes 6148
  84.2 62.7 %copy-start.59 = (f32[512]{0:T(512)}, f32[512]{0:T(512)S(1)}, u32[]{:S(2)}) copy-start(f32[512]{0:T(512)S(1)} %get-tuple-element.1028) | copy-start | bytes 6148
  85.0 70.2 %copy-start.48 = (f32[2048]{0:T(1024)}, f32[2048]{0:T(1024)S(1)}, u32[]{:S(2)}) copy-start(f32[2048]{0:T(1024)S(1)} %get-tuple-element.818) | copy-start | bytes 24580
  85.0 830.2 %copy-start.46 = (f32[2048]{0:T(1024)}, f32[2048]{0:T(1024)S(1)}, u32[]{:S(2)}) copy-start(f32[2048]{0:T(1024)S(1)} %get-tuple-element.817) | copy-start | bytes 24580
  86.9 63.0 %copy-start.35 = (f32[512,64]{1,0:T(8,128)}, f32[512,64]{1,0:T(8,128)S(1)}, u32[]{:S(2)}) copy-start(f32[512,64]{1,0:T(8,128)S(1)} %get-tuple-element.1014) | copy-start | bytes 393220
  89.1 66.1 %copy-start.69 = (f32[512]{0:T(512)}, f32[512]{0:T(512)S(1)}, u32[]{:S(2)}) copy-start(f32[512]{0:T(512)S(1)} %add_rsqrt_fusion) | copy-start | bytes 6148
  154.9 91.7 %all-gather.19.cloned.1.call-start = ((), (), s32[]{:S(2)}) async-start(), calls=%async_computation.18 | async-start | bytes 4718592 | tf_op jit(solution)/shard_map/all_gather | solution.py:379
  159.4 285.2 %all-gather.21.cloned.1.call-start = ((), (), s32[]{:S(2)}) async-start(), calls=%async_computation.19 | async-start | bytes 2359296 | tf_op jit(solution)/shard_map/all_gather | solution.py:363
  160.0 339.4 %all-gather.31.cloned.1.call-start = ((), (), s32[]{:S(2)}) async-start(), calls=%async_computation.25 | async-start | bytes 4718592 | tf_op jit(solution)/shard_map/all_gather | solution.py:364
  160.6 363.4 %all-gather.23.cloned.1.call-start = ((), (), s32[]{:S(2)}) async-start(), calls=%async_computation.20 | async-start | bytes 4718592 | tf_op jit(solution)/shard_map/all_gather | solution.py:394
  447.6 30.2 %copy-start.19 = (bf16[128,2048]{1,0:T(8,128)(2,1)S(1)}, bf16[128,2048]{1,0:T(8,128)(2,1)}, u32[]{:S(2)}) copy-start(bf16[128,2048]{1,0:T(8,128)(2,1)} %param.38) | copy-start | bytes 1572868
  478.7 436.5 %copy-start.4 = (f32[128,2048]{1,0:T(8,128)}, f32[128,2048]{1,0:T(8,128)S(1)}, u32[]{:S(2)}) copy-start(f32[128,2048]{1,0:T(8,128)S(1)} %get-tuple-element.904) | copy-start | bytes 3145732
  478.7 436.5 %copy-start.62 = (f32[128]{0:T(128)}, f32[128]{0:T(128)S(1)}, u32[]{:S(2)}) copy-start(f32[128]{0:T(128)S(1)} %add_rsqrt_fusion.2) | copy-start | bytes 1540
  479.9 132.3 %all-gather.25.cloned.1.call-start = ((), (), s32[]{:S(2)}) async-start(), calls=%async_computation.21 | async-start | bytes 10485760 | tf_op jit(solution)/shard_map/all_gather | solution.py:414
  480.6 220.9 %all-gather.27.cloned.1.call-start = ((), (), s32[]{:S(2)}) async-start(), calls=%async_computation.22 | async-start | bytes 10485760 | tf_op jit(solution)/shard_map/all_gather | solution.py:415
  481.4 309.4 %all-gather.29.cloned.1.call-start = ((), (), s32[]{:S(2)}) async-start(), calls=%async_computation.23 | async-start | bytes 10485760 | tf_op jit(solution)/shard_map/all_gather | solution.py:416
  482.0 430.9 %reduce-scatter.13.cloned.1.call-start = ((), (), s32[]{:S(2)}) async-start(), calls=%async_computation.26 | async-start | bytes 4718592 | tf_op jit(solution)/shard_map/reduce_scatter | solution.py:449
  499.4 357.4 %copy-start.44 = (s32[2,8,128]{2,0,1:T(2,128)}, s32[2,8,128]{2,0,1:T(2,128)S(1)}, u32[]{:S(2)}) copy-start(s32[2,8,128]{2,0,1:T(2,128)S(1)} %copy.491) | copy-start | bytes 24580
  864.3 10.4 all-to-all-start.2
  868.9 83.0 %all-gather.33.cloned.1.call-start = ((), (), s32[]{:S(2)}) async-start(), calls=%async_computation.27 | async-start | bytes 2621440 | tf_op jit(solution)/shard_map/all_gather | solution.py:472
  874.7 48.0 %copy-start.54 = (bf16[128,16]{0,1:T(8,128)(2,1)}, bf16[128,16]{0,1:T(8,128)(2,1)S(1)}, u32[]{:S(2)}) copy-start(bf16[128,16]{0,1:T(8,128)(2,1)S(1)} %multiply_convert_fusion.4) | copy-start | bytes 12292
  918.4 445.0 %reduce-scatter.15.cloned.1.call-start = ((), (), s32[]{:S(2)}) async-start(), calls=%async_computation.28 | async-start | bytes 4718592 | tf_op jit(solution)/shard_map/reduce_scatter | solution.py:498
  924.1 32.7 %copy-start.34 = (f32[512,4]{1,0:T(8,128)S(1)}, f32[512,4]{1,0:T(8,128)}, u32[]{:S(2)}) copy-start(f32[512,4]{1,0:T(8,128)} %copy-done.33) | copy-start | bytes 24580
  1301.8 99.6 %reduce-scatter.17.cloned.1.call-start = ((), (), s32[]{:S(2)}) async-start(), calls=%async_computation.29 | async-start | bytes 4718592 | tf_op jit(solution)/shard_map/reduce_scatter | solution.py:499
  1318.4 125.4 %reduce-scatter.21.cloned.1.call-start = ((), (), s32[]{:S(2)}) async-start(), calls=%async_computation.31 | async-start | bytes 2359296 | tf_op jit(solution)/shard_map/reduce_scatter | solution.py:475
  1322.8 221.3 %reduce-scatter.29.cloned.1.call-start = ((), (), s32[]{:S(2)}) async-start(), calls=%async_computation.35 | async-start | bytes 10485760 | tf_op jit(solution)/shard_map/reduce_scatter | solution.py:456
  1334.8 298.6 %reduce-scatter.25.cloned.1.call-start = ((), (), s32[]{:S(2)}) async-start(), calls=%async_computation.33 | async-start | bytes 10485760 | tf_op jit(solution)/shard_map/reduce_scatter | solution.py:456
  1348.1 374.5 %reduce-scatter.27.cloned.1.call-start = ((), (), s32[]{:S(2)}) async-start(), calls=%async_computation.34 | async-start | bytes 10485760 | tf_op jit(solution)/shard_map/reduce_scatter | solution.py:456
  1361.4 433.3 %reduce-scatter.19.cloned.1.call-start = ((), (), s32[]{:S(2)}) async-start(), calls=%async_computation.30 | async-start | bytes 7077888 | tf_op jit(solution)/shard_map/reduce_scatter | solution.py:546
  1424.7 420.6 %reduce-scatter.11.cloned.1.call-start = ((), (), s32[]{:S(2)}) async-start(), calls=%async_computation.24 | async-start | bytes 4718592 | tf_op jit(solution)/shard_map/reduce_scatter | solution.py:428
  1438.9 288.1 %all-to-all-start.3 = ((bf16[4,128,2048]{2,1,0:T(8,128)(2,1)}), bf16[4,128,2048]{2,1,0:T(8,128)(2,1)}, u32[]{:S(2)}, u32[]{:S(2)}) async-start(bf16[4,128,2048]{2,1,0:T(8,128)(2,1)} %bitcast.192), calls=%async_computation.7 | async-start | bytes 4194304 | tf_op jit(solution)/shard_map/all_to_all | solution.py:526
  1443.5 538.3 %reduce-scatter.23.cloned.1.call-start = ((), (), s32[]{:S(2)}) async-start(), calls=%async_computation.32 | async-start | bytes 270336 | tf_op jit(solution)/shard_map/reduce_scatter | solution.py:570
  1637.4 91.7 %copy-start.20 = (bf16[128,2048]{1,0:T(8,128)(2,1)S(1)}, bf16[128,2048]{1,0:T(8,128)(2,1)}, u32[]{:S(2)}) copy-start(bf16[128,2048]{1,0:T(8,128)(2,1)} %param.38) | copy-start | bytes 1572868
  1637.4 92.0 %copy-start.56 = (f32[2048]{0:T(1024)S(1)}, f32[2048]{0:T(1024)}, u32[]{:S(2)}) copy-start(f32[2048]{0:T(1024)} %get-tuple-element.809) | copy-start | bytes 24580
  1729.4 115.9 %copy-start.5 = (f32[128,2048]{1,0:T(8,128)S(1)}, f32[128,2048]{1,0:T(8,128)}, u32[]{:S(2)}) copy-start(f32[128,2048]{1,0:T(8,128)} %copy-done.4) | copy-start | bytes 3145732
  1729.4 115.9 %copy-start.15 = (f32[128,2048]{1,0:T(8,128)S(1)}, f32[128,2048]{1,0:T(8,128)}, u32[]{:S(2)}) copy-start(f32[128,2048]{1,0:T(8,128)} %copy-done.14) | copy-start | bytes 3145732
  1729.4 115.9 %copy-start.47 = (f32[2048]{0:T(1024)S(1)}, f32[2048]{0:T(1024)}, u32[]{:S(2)}) copy-start(f32[2048]{0:T(1024)} %copy-done.46) | copy-start | bytes 24580
  1729.4 115.9 %copy-start.63 = (f32[128]{0:T(128)S(1)}, f32[128]{0:T(128)}, u32[]{:S(2)}) copy-start(f32[128]{0:T(128)} %copy-done.62) | copy-start | bytes 1540
  1729.4 115.9 %copy-start.68 = (f32[128]{0:T(128)S(1)}, f32[128]{0:T(128)}, u32[]{:S(2)}) copy-start(f32[128]{0:T(128)} %copy-done.67) | copy-start | bytes 1540
  1797.5 186.6 %all-to-all-start.4 = ((bf16[3,256,512]{2,0,1:T(4,128)(2,1)}), bf16[3,256,512]{2,0,1:T(4,128)(2,1)}, u32[]{:S(2)}, u32[]{:S(2)}) async-start(bf16[3,256,512]{2,0,1:T(4,128)(2,1)} %copy.511), calls=%async_computation.9 | async-start | bytes 2097152 | tf_op jit(solution)/shard_map/all_to_all | solution.py:547
  (92 other events, 598.2 us)
Sparse Core Ops, SparseCore 0:
  9.8 43.2 all-gather.12
  55.4 65.0 all-gather.14
  155.0 43.8 all-gather.16
  200.9 45.6 all-gather.18
  248.1 27.9 all-gather.20
  277.5 46.2 all-gather.30
  480.0 43.9 all-gather.22
  525.9 86.2 all-gather.24
  614.0 87.4 all-gather.26
  703.2 87.4 all-gather.28
  862.8 50.0 reduce-scatter.12
  918.5 33.3 all-gather.32
  1301.9 48.2 reduce-scatter.14
  1353.0 48.3 reduce-scatter.16
  1404.1 34.5 reduce-scatter.20
  1441.6 102.4 reduce-scatter.28
  1547.0 86.2 reduce-scatter.24
  1636.3 86.3 reduce-scatter.26
  1724.9 69.7 reduce-scatter.18
  1796.8 48.3 reduce-scatter.10
  1848.1 133.6 reduce-scatter.22
